TPU v7x, 128 devices: a whole 4x4x4 slice. The times are simulated.
128 devices in a mesh: dp: 4 (over z), expert: 32 (over x, y, core).
Axes of the slice: x: 4, y: 4, z: 4, core: 2. Of those that a mesh axis runs over, the one named last changes fastest.
Arguments:
- tokens: bfloat16 [4096, 4096], P(('dp', 'expert')), may hold values from -6 to 6
- cotangent: bfloat16 [4096, 4096], P(('dp', 'expert')), may hold values from -6 to 6
- start: bfloat16 [4096, 4096], P(('dp', 'expert')), may hold values from -64 to 64
- gates: float32 [4096, 8], P(('dp', 'expert')), may hold values from 0.05 to 0.45
- routes: int32 [4096, 8], P(('dp', 'expert')), may hold values from 0 to 127, all different within a row; in each aligned block of 32 rows (0 to 31, 32 to 63, ...) at most 3 rows name the same one
- w_gate: bfloat16 [128, 4096, 768], P(('dp', 'expert')), may hold values from -0.09375 to 0.09375
- w_up: bfloat16 [128, 4096, 768], P(('dp', 'expert')), may hold values from -1 to 1
- w_down: bfloat16 [128, 768, 4096], P(('dp', 'expert')), may hold values from -2 to 2
Outputs:
- basis: bfloat16 [4096, 4096], P(('dp', 'expert'))
- residual: float32 [4096, 4096], P(('dp', 'expert'))
- tridiagonal: float32 [4], replicated
Inputs may be any that keep to these rules, and one draw needn't show every extreme that they name: `routes`: each token names 8 different experts; among the 32 tokens of one device (aligned blocks) no expert is named more than 3 times, a bound that some block reaches.
All inputs are finite; a program needn't handle non-finite values.
Results may differ from a plain program's by a relative error of at most 0.0074.
Values may be sent and summed in bfloat16 or wider, within the bound.
A program may use at most 128 MiB of HBM per device.

v0:
```python
import jax
import jax.numpy as jnp
from jax import lax
from jax.sharding import PartitionSpec as P

EPSILON = 1e-06


def silu_slopes(pre_gate):
    logistic = jax.nn.sigmoid(pre_gate)
    slope_one = logistic * (1.0 + pre_gate * (1.0 - logistic))
    slope_two = logistic * (1.0 - logistic) * (2.0 + pre_gate * (1.0 - 2.0 * logistic))
    return (slope_one, slope_two)


def flatten_four(block):
    shape = block.shape
    return block.reshape(shape[0] * shape[1] * shape[2], shape[3])


def send_inputs(block):
    moved = lax.all_to_all(
        flatten_four(block), ("dp", "expert"), split_axis=0, concat_axis=0, tiled=True
    )
    return moved.reshape(block.shape)


def send_rows(block):
    moved = lax.all_to_all(
        flatten_four(block), ("dp", "expert"), split_axis=0, concat_axis=0, tiled=True
    )
    return moved.reshape(block.shape)


def send_back(block):
    moved = lax.all_to_all(
        flatten_four(block), ("dp", "expert"), split_axis=0, concat_axis=0, tiled=True
    )
    return moved.reshape(block.shape)


def curvature_sum(left_vec, right_vec):
    return lax.psum(jnp.sum(left_vec * right_vec), ("dp", "expert"))


def residual_sum(vector):
    return lax.psum(jnp.sum(vector * vector), ("dp", "expert"))


def on_device(tokens, cotangent, start, gates, routes, w_gate, w_up, w_down):
    data_groups = lax.axis_size("dp")
    owner_groups = lax.axis_size("expert")
    device_count = data_groups * owner_groups
    tok_rows, width = tokens.shape
    chosen = routes.shape[1]
    capacity = 3 * tok_rows * chosen // (2 * device_count)
    slot_count = device_count * capacity
    pair_count = tok_rows * chosen
    flat_ids = routes.reshape(pair_count)
    columns = jnp.arange(device_count, dtype=jnp.int32)
    onehot = (flat_ids[:, None] == columns[None, :]).astype(jnp.bfloat16)
    order = jnp.arange(pair_count, dtype=jnp.int32)
    earlier = (order[:, None] > order[None, :]).astype(jnp.bfloat16)
    before = jnp.dot(earlier, onehot, preferred_element_type=jnp.float32)
    rank = jnp.sum(before * onehot.astype(jnp.float32), axis=1).astype(jnp.int32)
    slot = flat_ids * capacity + rank
    places = jnp.arange(slot_count, dtype=jnp.int32)
    select = places[:, None] == slot[None, :]
    pick = jnp.any(select.reshape(slot_count, tok_rows, chosen), axis=2).astype(jnp.bfloat16)
    slot_gate = jnp.sum(jnp.where(select, gates.reshape(pair_count)[None, :], 0.0), axis=1)

    def dispatch(vector):
        return jnp.dot(pick, vector, preferred_element_type=jnp.float32)

    x_send = dispatch(tokens).astype(jnp.bfloat16)
    c_send = (dispatch(cotangent) * slot_gate[:, None]).astype(jnp.bfloat16)
    packed = jnp.concatenate([x_send, c_send], axis=1).reshape(
        data_groups, owner_groups, capacity, 2 * width
    )
    arrived = send_inputs(packed).reshape(slot_count, 2 * width)
    x_rows = arrived[:, :width]
    c_rows = arrived[:, width:]
    gate_w = w_gate[0]
    up_w = w_up[0]
    down_w = w_down[0]
    pre_gate = jnp.dot(x_rows, gate_w, preferred_element_type=jnp.float32)
    pre_up = jnp.dot(x_rows, up_w, preferred_element_type=jnp.float32)
    back_grad = jnp.einsum("sd,fd->sf", c_rows, down_w, preferred_element_type=jnp.float32)
    slope_one, slope_two = silu_slopes(pre_gate)
    scale_one = back_grad * slope_one
    scale_two = back_grad * pre_up * slope_two

    def hessian_product(vector):
        outgoing = (
            dispatch(vector)
            .astype(jnp.bfloat16)
            .reshape(data_groups, owner_groups, capacity, width)
        )
        rows_in = send_rows(outgoing).reshape(slot_count, width)
        along_gate = jnp.dot(rows_in, gate_w, preferred_element_type=jnp.float32)
        along_up = jnp.dot(rows_in, up_w, preferred_element_type=jnp.float32)
        out_gate = (scale_one * along_up + scale_two * along_gate).astype(jnp.bfloat16)
        out_up = (scale_one * along_gate).astype(jnp.bfloat16)
        summed = jnp.einsum(
            "sf,df->sd", out_gate, gate_w, preferred_element_type=jnp.float32
        ) + jnp.einsum("sf,df->sd", out_up, up_w, preferred_element_type=jnp.float32)
        result = summed.astype(jnp.bfloat16).reshape(data_groups, owner_groups, capacity, width)
        returned = send_back(result).reshape(slot_count, width)
        return jnp.einsum("st,sd->td", pick, returned, preferred_element_type=jnp.float32)

    entry_total = float(device_count * tok_rows * width)
    anchor = start.astype(jnp.float32)
    anchor_square = lax.psum(jnp.sum(anchor * anchor), ("dp", "expert")) / entry_total
    anchor_norm = jnp.sqrt(anchor_square + EPSILON)
    base = anchor / anchor_norm
    image_zero = hessian_product(start)
    alpha_zero = curvature_sum(anchor, image_zero) / entry_total / (anchor_norm * anchor_norm)
    first_resid = image_zero / anchor_norm - alpha_zero * base
    beta_one = jnp.sqrt(residual_sum(first_resid) / entry_total + EPSILON)
    basis = (first_resid / beta_one).astype(jnp.bfloat16)
    image_one = hessian_product(basis)
    basis_wide = basis.astype(jnp.float32)
    alpha_one = curvature_sum(basis_wide, image_one) / entry_total
    residual = image_one - alpha_one * basis_wide - beta_one * base
    beta_two = jnp.sqrt(residual_sum(residual) / entry_total + EPSILON)
    return (basis, residual, jnp.stack([alpha_zero, beta_one, alpha_one, beta_two]))


def solution(mesh):
    in_specs = (
        P(("dp", "expert"), None),
        P(("dp", "expert"), None),
        P(("dp", "expert"), None),
        P(("dp", "expert"), None),
        P(("dp", "expert"), None),
        P(("dp", "expert"), None, None),
        P(("dp", "expert"), None, None),
        P(("dp", "expert"), None, None),
    )
    out_specs = (P(("dp", "expert"), None), P(("dp", "expert"), None), P())
    return jax.shard_map(
        on_device, mesh=mesh, in_specs=in_specs, out_specs=out_specs, check_vma=False
    )
```

profile of v0, /device:TPU:1, one launch (start us, length us, event | category | flops | bytes accessed | tf_op | source)
XLA Modules:
  0.0 746.3 jit_solution(9067182088560946235)
XLA Ops:
  0.6 0.8 copy.15
  1.5 0.1 eq.36
  1.5 0.2 fusion.61
  1.8 0.1 convert_element_type.61
  1.9 0.2 fusion.67
  2.1 2.0 convolution_convert_fusion.1
  4.1 4.4 all_to_all.43
  8.5 12.0 %all-to-all-start.1 = ((bf16[128,3,4096]{2,1,0:T(4,128)(2,1)}), bf16[128,3,4096]{2,1,0:T(4,128)(2,1)}, u32[]{:S(2)}, u32[]{:S(2)}) async-start(bf16[128,3,4096]{2,1,0:T(4,128)(2,1)} %all_to_all.43), calls=%async_computation.1 | async-start | bytes 8388608 | tf_op jit(solution)/shard_map/all_to_all | solution.py:29
  20.6 0.1 broadcast_in_dim.20
  20.7 0.1 select_reduce_fusion
  20.8 1.0 convolution_convert_fusion.2
  21.9 1.0 multiply_convert_fusion
  22.9 3.3 pad_maximum_fusion
  26.2 12.8 %all_to_all.40 = bf16[128,3,8192]{2,1,0:T(4,128)(2,1)} reshape(bf16[384,8192]{1,0:T(8,128)(2,1)} %pad_maximum_fusion) | data formatting | bytes 12582912 | tf_op jit(solution)/shard_map/all_to_all | solution.py:22
  39.1 34.2 %all-to-all-done.1 = bf16[128,3,4096]{2,1,0:T(4,128)(2,1)} async-done(((bf16[128,3,4096]{2,1,0:T(4,128)(2,1)}), bf16[128,3,4096]{2,1,0:T(4,128)(2,1)}, u32[]{:S(2)}, u32[]{:S(2)}) %all-to-all-start.1) | async-done | bytes 3145760 | tf_op jit(solution)/shard_map/all_to_all | solution.py:29
  73.3 6.1 all-to-all-start
  79.4 6.0 all_to_all.45
  85.4 7.5 %fusion.16 = f32[384,768]{1,0:T(8,128)} fusion(bf16[384,4096]{1,0:T(8,128)(2,1)S(1)} %all_to_all.45, bf16[1,4096,768]{2,1,0:T(8,128)(2,1)} %param.13), kind=kOutput, calls=%fused_computation.17 | convolution fusion | flops 2415919104 | bytes 10616832 | tf_op jit(solution)/shard_map/dot_general | solution.py:100
  93.0 85.4 %all-to-all-done = bf16[128,3,8192]{2,1,0:T(4,128)(2,1)} async-done(((bf16[128,3,8192]{2,1,0:T(4,128)(2,1)}), bf16[128,3,8192]{2,1,0:T(4,128)(2,1)}, u32[]{:S(2)}, u32[]{:S(2)}) %all-to-all-start) | async-done | bytes 6291488 | tf_op jit(solution)/shard_map/all_to_all | solution.py:22
  178.4 13.9 %all_to_all.42 = bf16[384,8192]{1,0:T(8,128)(2,1)} reshape(bf16[128,3,8192]{2,1,0:T(4,128)(2,1)} %all-to-all-done) | data formatting | bytes 12582912 | tf_op jit(solution)/shard_map/all_to_all | solution.py:22
  192.3 6.5 fusion.18
  198.7 5.5 fusion.59
  204.3 3.8 fusion.40
  208.2 4.7 fusion.4
  212.9 16.3 %add_convert_fusion.1 = bf16[384,4096]{1,0:T(8,128)(2,1)} fusion(f32[384,4096]{1,0:T(8,128)} %fusion.4, bf16[1,4096,768]{2,1,0:T(8,128)(2,1)} %param.13, f32[384,768]{1,0:T(8,128)S(1)} %get-tuple-element.11, bf16[384,4096]{1,0:T(8,128)(2,1)} %copy-done.2, bf16[1,4096,768]{2,1,0:T(8,128)(2,1)} %param.14, f32[384,768]{1,0:T(8,128)} %fusion.40, ...), kind=kOutput, calls=%fused_computation.24 | convolution fusion | flops 4836163584 | bytes 28704768 | tf_op jit(solution)/shard_map/sf,df->sd/dot_general | solution.py:104
  229.2 7.1 all_to_all.46
  236.2 61.7 %all_to_all.60 = bf16[128,3,4096]{2,1,0:T(4,128)(2,1)} all-to-all(bf16[128,3,4096]{2,1,0:T(4,128)(2,1)} %all_to_all.46), channel_id=1, replica_groups=mesh['dp'=4,'expert'=32] {'dp','expert'}, dimensions={0} | all-to-all | bytes 6291456 | tf_op jit(solution)/shard_map/all_to_all | solution.py:36
  297.9 7.5 %all_to_all.48 = bf16[384,4096]{1,0:T(8,128)(2,1)} reshape(bf16[128,3,4096]{2,1,0:T(4,128)(2,1)} %all_to_all.60) | data formatting | bytes 6291456 | tf_op jit(solution)/shard_map/all_to_all | solution.py:36
  305.4 3.1 fusion.65
  308.5 62.7 %all-reduce = (f32[]{:T(128)}, f32[]{:T(128)}) all-reduce(f32[]{:T(128)} %get-tuple-element.4, f32[]{:T(128)} %get-tuple-element.3), channel_id=1, replica_groups=mesh['dp'=4,'expert'=32] {'dp','expert'}, use_global_device_ids=true, to_apply=%region_6.7 | all-reduce | flops 2 | bytes 16 | tf_op jit(solution)/shard_map/psum | solution.py:43
  372.6 0.7 multiply_reduce_fusion.1
  373.3 62.7 %psum.37 = f32[]{:T(128)} all-reduce(f32[]{:T(128)} %get-tuple-element.9), channel_id=1, replica_groups=mesh['dp'=4,'expert'=32] {'dp','expert'}, use_global_device_ids=true, to_apply=%region_8.9 | all-reduce | flops 1 | bytes 8 | tf_op jit(solution)/shard_map/psum | solution.py:47
  436.8 2.8 convolution_convert_fusion
  439.5 7.1 all_to_all.49
  446.6 58.8 %all_to_all.61 = bf16[128,3,4096]{2,1,0:T(4,128)(2,1)} all-to-all(bf16[128,3,4096]{2,1,0:T(4,128)(2,1)} %all_to_all.49), channel_id=1, replica_groups=mesh['dp'=4,'expert'=32] {'dp','expert'}, dimensions={0} | all-to-all | bytes 6291456 | tf_op jit(solution)/shard_map/all_to_all | solution.py:29
  505.4 7.6 %all_to_all.51 = bf16[384,4096]{1,0:T(8,128)(2,1)} reshape(bf16[128,3,4096]{2,1,0:T(4,128)(2,1)} %all_to_all.61) | data formatting | bytes 6291456 | tf_op jit(solution)/shard_map/all_to_all | solution.py:29
  512.9 6.5 fusion.12
  519.4 1.0 copy-done.5
  520.5 4.6 fusion
  525.0 16.3 %add_convert_fusion = bf16[384,4096]{1,0:T(8,128)(2,1)} fusion(f32[384,4096]{1,0:T(8,128)} %fusion, bf16[1,4096,768]{2,1,0:T(8,128)(2,1)} %param.13, f32[384,768]{1,0:T(8,128)S(1)} %get-tuple-element.11, bf16[384,4096]{1,0:T(8,128)(2,1)} %all_to_all.51, bf16[1,4096,768]{2,1,0:T(8,128)(2,1)} %param.14, f32[384,768]{1,0:T(8,128)} %fusion.40, ...), kind=kOutput, calls=%fused_computation.23 | convolution fusion | flops 4836163584 | bytes 28704768 | tf_op jit(solution)/shard_map/sf,df->sd/dot_general | solution.py:104
  541.3 7.1 all_to_all.52
  548.4 58.5 %all_to_all.62 = bf16[128,3,4096]{2,1,0:T(4,128)(2,1)} all-to-all(bf16[128,3,4096]{2,1,0:T(4,128)(2,1)} %all_to_all.52), channel_id=1, replica_groups=mesh['dp'=4,'expert'=32] {'dp','expert'}, dimensions={0} | all-to-all | bytes 6291456 | tf_op jit(solution)/shard_map/all_to_all | solution.py:36
  607.0 6.0 all_to_all.54
  613.0 3.0 fusion.62
  615.9 62.7 %psum.38 = f32[]{:T(128)} all-reduce(f32[]{:T(128)} %get-tuple-element.14), channel_id=1, replica_groups=mesh['dp'=4,'expert'=32] {'dp','expert'}, use_global_device_ids=true, to_apply=%region_10.11 | all-reduce | flops 1 | bytes 8 | tf_op jit(solution)/shard_map/psum | solution.py:43
  679.2 2.8 multiply_reduce_fusion
  682.1 62.7 %psum.39 = f32[]{:T(128)} all-reduce(f32[]{:T(128)} %get-tuple-element.7), channel_id=1, replica_groups=mesh['dp'=4,'expert'=32] {'dp','expert'}, use_global_device_ids=true, to_apply=%region_12.13 | all-reduce | flops 1 | bytes 8 | tf_op jit(solution)/shard_map/psum | solution.py:47
  745.4 0.6 pad_maximum_fusion.1
  (36 shorter events, 0.2 us)
Async XLA Ops:
  0.6 20.2 %copy-start = (bf16[32,4096]{1,0:T(8,128)(2,1)S(1)}, bf16[32,4096]{1,0:T(8,128)(2,1)}, u32[]{:S(2)}) copy-start(bf16[32,4096]{1,0:T(8,128)(2,1)} %param.8) | copy-start | bytes 786436
  8.5 12.0 %copy-start.10 = (f32[32,8]{0,1:T(8,128)S(1)}, f32[32,8]{0,1:T(8,128)}, u32[]{:S(2)}) copy-start(f32[32,8]{0,1:T(8,128)} %param.11) | copy-start | bytes 3076
  8.5 64.8 %all-to-all-start.1 = ((bf16[128,3,4096]{2,1,0:T(4,128)(2,1)}), bf16[128,3,4096]{2,1,0:T(4,128)(2,1)}, u32[]{:S(2)}, u32[]{:S(2)}) async-start(bf16[128,3,4096]{2,1,0:T(4,128)(2,1)} %all_to_all.43), calls=%async_computation.1 | async-start | bytes 8388608 | tf_op jit(solution)/shard_map/all_to_all | solution.py:29
  20.5 1.4 copy-start.9
  73.3 105.1 %all-to-all-start = ((bf16[128,3,8192]{2,1,0:T(4,128)(2,1)}), bf16[128,3,8192]{2,1,0:T(4,128)(2,1)}, u32[]{:S(2)}, u32[]{:S(2)}) async-start(bf16[128,3,8192]{2,1,0:T(4,128)(2,1)} %all_to_all.40), calls=%async_computation | async-start | bytes 16777216 | tf_op jit(solution)/shard_map/all_to_all | solution.py:22
  85.4 7.5 %copy-start.2 = (bf16[384,4096]{1,0:T(8,128)(2,1)}, bf16[384,4096]{1,0:T(8,128)(2,1)S(1)}, u32[]{:S(2)}) copy-start(bf16[384,4096]{1,0:T(8,128)(2,1)S(1)} %all_to_all.45) | copy-start | bytes 9437188
  178.4 25.9 %slice-start = ((s8[6291456]{0:T(1024)(128)(4,1)}), s8[2097152]{0:T(1024)(128)(4,1)S(1)}, s32[]{:S(2)}) async-start(s8[6291456]{0:T(1024)(128)(4,1)} %bitcast.85), calls=%async_computation.5 | async-start | bytes 4194304
  192.2 6.5 copy-start.3
  192.3 12.1 %slice-start.1 = ((s8[6291456]{0:T(1024)(128)(4,1)}), s8[4194304]{0:T(1024)(128)(4,1)S(1)}, s32[]{:S(2)}) async-start(s8[6291456]{0:T(1024)(128)(4,1)} %bitcast.85), calls=%async_computation.6 | async-start | bytes 8388608
  204.3 3.9 copy-start.4
  297.9 7.5 %copy-start.7 = (bf16[32,4096]{1,0:T(8,128)(2,1)S(1)}, bf16[32,4096]{1,0:T(8,128)(2,1)}, u32[]{:S(2)}) copy-start(bf16[32,4096]{1,0:T(8,128)(2,1)} %param.10) | copy-start | bytes 786436
  373.3 73.3 %copy-start.6 = (f32[32,4096]{1,0:T(8,128)}, f32[32,4096]{1,0:T(8,128)S(1)}, u32[]{:S(2)}) copy-start(f32[32,4096]{1,0:T(8,128)S(1)} %get-tuple-element.10) | copy-start | bytes 1572868
  436.8 9.9 %copy-start.8 = (bf16[32,4096]{1,0:T(8,128)(2,1)}, bf16[32,4096]{1,0:T(8,128)(2,1)S(1)}, u32[]{:S(2)}) copy-start(bf16[32,4096]{1,0:T(8,128)(2,1)S(1)} %divide_convert_fusion) | copy-start | bytes 786436
  505.4 15.1 %slice-start.2 = ((s8[6291456]{0:T(1024)(128)(4,1)}), s8[2097152]{0:T(1024)(128)(4,1)S(1)}, s32[]{:S(2)}) async-start(s8[6291456]{0:T(1024)(128)(4,1)} %bitcast.87), calls=%async_computation.7 | async-start | bytes 4194304
  512.9 7.5 %slice-start.3 = ((s8[6291456]{0:T(1024)(128)(4,1)}), s8[4194304]{0:T(1024)(128)(4,1)S(1)}, s32[]{:S(2)}) async-start(s8[6291456]{0:T(1024)(128)(4,1)} %bitcast.87), calls=%async_computation.8 | async-start | bytes 8388608
  519.4 1.0 copy-start.5
  607.0 139.1 %copy-start.1 = (bf16[32,4096]{1,0:T(8,128)(2,1)S(1)}, bf16[32,4096]{1,0:T(8,128)(2,1)}, u32[]{:S(2)}) copy-start(bf16[32,4096]{1,0:T(8,128)(2,1)} %param.8) | copy-start | bytes 786436
where the time goes:
time: 753 us; the launch traced here: 746 us
  blocking collectives  430 us (57%)
  waiting for transfers between devices  120 us (16%)
  matrix products  84.8 us (11%)
  local copies, waits for them, and re-layouts  81.6 us (11%)
  starting transfers between devices  18.1 us (2%)
  other arithmetic  7.9 us (1%)
    psum x2, blocking collectives, residual_sum(): return lax.psum(jnp.sum(vector * vector), ('dp', 'expert'))  125 us
    psum x2, blocking collectives, curvature_sum(): return lax.psum(jnp.sum(left_vec * right_vec), ('dp', 'expert'))  125 us
    all_to_all x2, blocking collectives, send_back(): lax.all_to_all(flatten_four(block), ('dp', 'expert'), split_axis=0, conca...  120 us
    all_to_all x1, waiting for transfers between devices, send_inputs(): lax.all_to_all(flatten_four(block), ('dp', 'expert'), split_axis=0, conca...  85.4 us
    all_to_all x1, blocking collectives, send_rows(): lax.all_to_all(flatten_four(block), ('dp', 'expert'), split_axis=0, conca...  58.8 us
    all_to_all x1, waiting for transfers between devices, send_rows(): lax.all_to_all(flatten_four(block), ('dp', 'expert'), split_axis=0, conca...  34.2 us
    dot_general x2, matrix products, hessian_product(): jnp.einsum('sf,df->sd', out_gate, gate_w, preferred_element_type=jnp.floa...  32.6 us
    all_to_all x4, local copies, waits for them, and re-layouts, send_back(): lax.all_to_all(flatten_four(block), ('dp', 'expert'), split_axis=0, conca...  27.6 us
  transfers between devices with their start and end apart: 2, of which 2 were waited for; matrix products, arithmetic and copies ran while one was open for 2% of the time, Pallas kernels for 0%

commit v1 on v0

v1 whole, which is shorter than its diff:
```python
import functools
import jax
import jax.numpy as jnp
from jax import lax
from jax.experimental import pallas as pl
from jax.experimental.pallas import tpu as pltpu
from jax.sharding import PartitionSpec as P

EPSILON = 1e-06
MESH = pl.DeviceIdType.MESH
F32 = jnp.float32
BF16 = jnp.bfloat16
SUB = 16
ORDERS = (("z", "x", "y"), ("x", "y", "z"), ("y", "z", "x"))
ANY = pl.BlockSpec(memory_space=pl.ANY)
VM = pl.BlockSpec(memory_space=pltpu.VMEM)


def rem(value, size):
    return lax.rem(value, jnp.int32(size))


def here():
    expert = lax.axis_index("expert")
    return {
        "z": lax.axis_index("dp"),
        "x": expert // 8,
        "y": rem(expert // 2, 4),
        "c": rem(expert, 2),
    }


def device_of(place):
    return (place["z"], place["x"] * 8 + place["y"] * 2 + place["c"])


def offsets(axes):
    if len(axes) == 1:
        return [(0,), (1,), (3,), (2,)]
    return [(0, 0), (0, 1), (1, 0), (3, 0), (1, 1), (3, 1), (2, 0), (2, 1)]


def size_of(axes):
    return 4 if len(axes) == 1 else 8


def index_of(place, axes):
    value = place[axes[0]]
    return value * 2 + place["c"] if len(axes) == 2 else value


def moved(place, axes, step, sign=1):
    new = dict(place)
    for axis, amount in zip(axes, step):
        count = 2 if axis == "c" else 4
        new[axis] = rem(place[axis] + (amount if sign > 0 else count - amount), count)
    return new


def slot_id(axes, step):
    return step[0] * 2 + step[1] if len(axes) == 2 else step[0]


def groups_of(order, back):
    first, second, third = (order[0],), (order[1],), (order[2], "c")
    return (third, second, first) if back else (first, second, third)


def peers_of(place):
    found = []
    for axis in ("z", "x", "y"):
        for amount in (1, 2, 3):
            near = moved(place, (axis,), (amount,))
            found.append(near)
            found.append(moved(near, ("c",), (1,)))
    found.append(moved(place, ("c",), (1,)))
    return found


def entry_barrier(places):
    barrier = pltpu.get_barrier_semaphore()
    for place in places:
        pl.semaphore_signal(barrier, inc=1, device_id=device_of(place), device_id_type=MESH)
    pl.semaphore_wait(barrier, len(places))


REDUCE_GROUPS = (("z",), ("x",), ("y", "c"))


class Reduction:
    def __init__(self, place, tiles, send_sem, recv_sem):
        self.place, self.tiles = place, tiles
        self.send_sem, self.recv_sem = send_sem, recv_sem

    def send(self, level, value):
        axes, place = REDUCE_GROUPS[level], self.place
        tile = self.tiles[level]
        mine = index_of(place, axes)
        tile[mine] = value
        for step in offsets(axes)[1:]:
            pltpu.make_async_remote_copy(
                tile.at[mine],
                tile.at[mine],
                self.send_sem.at[level],
                self.recv_sem.at[level],
                device_id=device_of(moved(place, axes, step)),
                device_id_type=MESH,
            ).start()

    def receive(self, level):
        axes, place = REDUCE_GROUPS[level], self.place
        tile = self.tiles[level]
        count = size_of(axes)
        rest = tile.at[pl.ds(0, count - 1)]
        bulk = pltpu.make_async_remote_copy(
            rest,
            rest,
            self.send_sem.at[level],
            self.recv_sem.at[level],
            device_id=device_of(moved(place, axes, offsets(axes)[1])),
            device_id_type=MESH,
        )
        bulk.wait_send()
        bulk.wait_recv()
        total = tile[0]
        for index in range(1, count):
            total = total + tile[index]
        return total


def reduction_scratch():
    return [
        pltpu.VMEM((4, 8, 128), F32),
        pltpu.VMEM((4, 8, 128), F32),
        pltpu.VMEM((8, 8, 128), F32),
        pltpu.SemaphoreType.DMA((3,)),
        pltpu.SemaphoreType.DMA((3,)),
    ]


def exchange_kernel(back, summing, *refs):
    blocks = refs[:3]
    refs = refs[3:]
    if summing:
        part, refs = refs[0], refs[1:]
    outs, refs = refs[:3], refs[3:]
    if summing:
        total, refs = refs[0], refs[1:]
    first_hold, second_hold, refs = refs[:3], refs[3:6], refs[6:]
    (send_one, send_two, send_three, recv_one, recv_two, recv_three, local_one, local_two, local_three) = refs[:9]
    place = here()
    plans = [groups_of(order, back) for order in ORDERS]
    if summing:
        tiles, (sum_send, sum_recv) = refs[9:12], refs[12:14]
        reduction = Reduction(place, tiles, sum_send, sum_recv)
    entry_barrier(peers_of(place))

    def remote(src, dst, send_sem, recv_sem, target):
        return pltpu.make_async_remote_copy(
            src, dst, send_sem, recv_sem, device_id=device_of(target), device_id_type=MESH
        )

    if summing:
        reduction.send(0, part[...])
    for turn in range(8):
        for r, (one, two, three) in enumerate(plans):
            if turn >= size_of(one):
                continue
            step = offsets(one)[turn]
            mine = index_of(place, one)
            if turn == 0:
                pltpu.make_async_copy(blocks[r].at[mine], first_hold[r].at[mine], local_one.at[r]).start()
                continue
            target = moved(place, one, step)
            remote(
                blocks[r].at[index_of(target, one)],
                first_hold[r].at[mine],
                send_one.at[r],
                recv_one.at[r, slot_id(one, step)],
                target,
            ).start()
    for turn in range(8):
        for r, (one, two, three) in enumerate(plans):
            if turn >= size_of(one):
                continue
            step = offsets(one)[turn]
            mine_one, mine_two = index_of(place, one), index_of(place, two)
            if turn == 0:
                source = mine_one
                pltpu.make_async_copy(blocks[r].at[source], first_hold[r].at[source], local_one.at[r]).wait()
            else:
                origin = moved(place, one, step, -1)
                source = index_of(origin, one)
                held = first_hold[r].at[source]
                remote(held, held, send_one.at[r], recv_one.at[r, slot_id(one, step)], origin).wait_recv()
            for hop in offsets(two)[1:]:
                target = moved(place, two, hop)
                remote(
                    first_hold[r].at[source, index_of(target, two)],
                    second_hold[r].at[mine_two, source],
                    send_two.at[r],
                    recv_two.at[r, slot_id(two, hop)],
                    target,
                ).start()
            pltpu.make_async_copy(
                first_hold[r].at[source, mine_two], second_hold[r].at[mine_two, source], local_two.at[r]
            ).start()
    if summing:
        reduction.send(1, reduction.receive(0))
    for turn in range(4):
        for r, (one, two, three) in enumerate(plans):
            step = offsets(two)[turn]
            mine_two, mine_three = index_of(place, two), index_of(place, three)
            if turn == 0:
                source = mine_two
                held = second_hold[r].at[source]
                pltpu.make_async_copy(held, held, local_two.at[r]).wait()
            else:
                origin = moved(place, two, step, -1)
                source = index_of(origin, two)
                held = second_hold[r].at[source]
                remote(held, held, send_two.at[r], recv_two.at[r, slot_id(two, step)], origin).wait_recv()
            for hop in offsets(three)[1:]:
                target = moved(place, three, hop)
                remote(
                    second_hold[r].at[source, :, index_of(target, three)],
                    outs[r].at[mine_three, source],
                    send_three.at[r],
                    recv_three.at[r],
                    target,
                ).start()
            pltpu.make_async_copy(
                second_hold[r].at[source, :, mine_three], outs[r].at[mine_three, source], local_three.at[r]
            ).start()
    if summing:
        reduction.send(2, reduction.receive(1))
        total[...] = reduction.receive(2)
    near = moved(place, ("c",), (1,))
    for r, (one, two, three) in enumerate(plans):
        rest = blocks[r].at[pl.ds(0, size_of(one) - 1)]
        remote(rest, rest, send_one.at[r], recv_three.at[r], near).wait_send()
        rest = second_hold[r].at[pl.ds(0, 3)]
        remote(rest, rest, send_two.at[r], recv_three.at[r], near).wait_send()
        rest = outs[r].at[pl.ds(0, size_of(three) - 1)]
        bulk = remote(rest, rest, send_three.at[r], recv_three.at[r], near)
        bulk.wait_send()
        bulk.wait_recv()
        mine = outs[r].at[index_of(place, three)]
        pltpu.make_async_copy(mine, mine, local_three.at[r]).wait()


def exchange(blocks, back, number, part=None):
    sub, lanes = blocks[0].shape[1:]
    dims_in = (8, 4, 4) if back else (4, 4, 8)
    dims_out = dims_in[::-1]
    one, two, three = dims_in
    summing = part is not None
    scratch = [pltpu.VMEM((one, two, three, sub, lanes), BF16)] * 3
    scratch += [pltpu.VMEM((two, one, three, sub, lanes), BF16)] * 3
    scratch += [pltpu.SemaphoreType.DMA((3,))] * 3
    scratch += [pltpu.SemaphoreType.DMA((3, 8))] * 2
    scratch += [pltpu.SemaphoreType.DMA((3,))] * 4
    out_shape = [jax.ShapeDtypeStruct(dims_out + (sub, lanes), BF16)] * 3
    operands = [block.reshape(dims_in + (sub, lanes)) for block in blocks]
    in_specs, out_specs = [ANY] * 3, [ANY] * 3
    if summing:
        operands.append(part)
        in_specs.append(VM)
        out_specs.append(VM)
        out_shape.append(jax.ShapeDtypeStruct((8, 128), F32))
        scratch += reduction_scratch()
    results = pl.pallas_call(
        functools.partial(exchange_kernel, back, summing),
        out_shape=out_shape,
        in_specs=in_specs,
        out_specs=out_specs,
        scratch_shapes=scratch,
        name="exchange_%d" % number,
        compiler_params=pltpu.CompilerParams(
            collective_id=number, has_side_effects=True, vmem_limit_bytes=48 << 20
        ),
    )(*operands)
    moved_blocks = [result.reshape(128, sub, lanes) for result in results[:3]]
    return (moved_blocks, results[3]) if summing else moved_blocks


def swap_matrix():
    row = lax.broadcasted_iota(jnp.int32, (256, 256), 0)
    column = lax.broadcasted_iota(jnp.int32, (256, 256), 1)
    hit = (row // 16 == rem(column, 16)) & (rem(row, 16) == column // 16)
    return hit.astype(F32).astype(BF16)


def pack(rows_ref, row_start, swap, out_ref, lane):
    def block(index, carry):
        start = pl.multiple_of(row_start + index * 16, 16)
        stacked = jnp.concatenate(
            [rows_ref[pl.ds(start, 16), j * 256 : (j + 1) * 256] for j in range(SUB)], axis=0
        )
        turned = jnp.dot(swap, stacked, preferred_element_type=F32).astype(BF16)
        out_ref[pl.ds(pl.multiple_of(index * 16, 16), 16), :, lane : lane + 256] = turned.reshape(16, 16, 256)
        return carry

    lax.fori_loop(0, 8, block, 0)


def unpack(in_ref, lane, swap, rows_ref, row_start):
    def block(index, carry):
        stacked = in_ref[pl.ds(pl.multiple_of(index * 16, 16), 16), :, lane : lane + 256].reshape(256, 256)
        turned = jnp.dot(swap, stacked, preferred_element_type=F32).astype(BF16)
        start = pl.multiple_of(row_start + index * 16, 16)
        for j in range(SUB):
            rows_ref[pl.ds(start, 16), j * 256 : (j + 1) * 256] = turned[j * 16 : (j + 1) * 16, :]
        return carry

    lax.fori_loop(0, 8, block, 0)


def expert_ids(order):
    position = lax.broadcasted_iota(jnp.int32, (128, 32), 0)
    value = {
        order[0]: position // 32,
        order[1]: rem(position // 8, 4),
        order[2]: rem(position // 2, 4),
    }
    return value["z"] * 32 + value["x"] * 8 + value["y"] * 2 + rem(position, 2)


def send_kernel(routes, gates, tokens, cotangent, start, out_a, out_b, out_c, pick_ref, rows):
    swap = swap_matrix()
    early = lax.broadcasted_iota(jnp.int32, (32, 32), 0) < lax.broadcasted_iota(jnp.int32, (32, 32), 1)
    early = early.astype(F32).astype(BF16)
    for r, out in enumerate((out_a, out_b, out_c)):
        ids = expert_ids(ORDERS[r])
        named = jnp.zeros((128, 32), F32)
        weight = jnp.zeros((128, 32), F32)
        for k in range(8):
            hit = routes[k : k + 1, :] == ids
            named = named + hit.astype(F32)
            weight = weight + jnp.where(hit, gates[k : k + 1, :], 0.0)
        before = jnp.dot(named.astype(BF16), early, preferred_element_type=F32)
        keep = (named > 0.5) & (before == float(r))
        pick = keep.astype(F32).astype(BF16)
        pick_ref[r] = pick
        slot_gate = jnp.sum(jnp.where(keep, weight, 0.0), axis=1, keepdims=True)
        for unit, source in enumerate((tokens, cotangent, start)):
            for part in range(4):
                columns = slice(part * 1024, (part + 1) * 1024)
                picked = jnp.dot(pick, source[:, columns], preferred_element_type=F32)
                if unit == 1:
                    picked = picked * slot_gate
                rows[:, columns] = picked.astype(BF16)
            pack(rows, 0, swap, out, unit * 256)


def send_messages(routes, gates, tokens, cotangent, start):
    message = jax.ShapeDtypeStruct((128, SUB, 768), BF16)
    return pl.pallas_call(
        send_kernel,
        out_shape=[message] * 3 + [jax.ShapeDtypeStruct((3, 128, 32), BF16)],
        in_specs=[VM] * 5,
        out_specs=[VM] * 4,
        scratch_shapes=[pltpu.VMEM((128, 4096), BF16)],
        name="send_messages",
        compiler_params=pltpu.CompilerParams(vmem_limit_bytes=32 << 20),
    )(routes.T, gates.T, tokens, cotangent, start)


CONTRACT_LAST = (((1,), (1,)), ((), ()))


def last_dot(left, right):
    return lax.dot_general(left, right, CONTRACT_LAST, preferred_element_type=F32)


def results_out(out_gate, out_up, gate_w, up_w, rows, swap, outs):
    def tile(index, carry):
        start = pl.multiple_of(index * 256, 256)
        summed = last_dot(out_gate[...], gate_w[pl.ds(start, 256), :])
        summed = summed + last_dot(out_up[...], up_w[pl.ds(start, 256), :])
        rows[:, pl.ds(start, 256)] = summed.astype(BF16)
        return carry

    lax.fori_loop(0, 16, tile, 0)
    for r in range(3):
        pack(rows, r * 128, swap, outs[r], 0)


def first_expert_kernel(
    in_a, in_b, in_c, gate_h, up_h, down_h, out_a, out_b, out_c, one_ref, two_ref, ag_ref, au_ref,
    gate_w, up_w, down_w, x_rows, c_rows, v_rows, out_gate, out_up, sems,
):
    copies = [
        pltpu.make_async_copy(src, dst, sems.at[i])
        for i, (src, dst) in enumerate(((gate_h, gate_w), (up_h, up_w), (down_h, down_w)))
    ]
    for copy in copies:
        copy.start()
    swap = swap_matrix()
    for r, source in enumerate((in_a, in_b, in_c)):
        for unit, rows in enumerate((x_rows, c_rows, v_rows)):
            unpack(source, unit * 256, swap, rows, r * 128)
    for copy in copies:
        copy.wait()

    def tile(index, carry):
        columns = pl.ds(pl.multiple_of(index * 256, 256), 256)
        gate_t, up_t = gate_w[:, columns], up_w[:, columns]
        pre_gate = jnp.dot(x_rows[...], gate_t, preferred_element_type=F32)
        pre_up = jnp.dot(x_rows[...], up_t, preferred_element_type=F32)
        back_grad = last_dot(c_rows[...], down_w[columns, :])
        logistic = 1.0 / (1.0 + jnp.exp(-pre_gate))
        slope_one = logistic * (1.0 + pre_gate * (1.0 - logistic))
        slope_two = logistic * (1.0 - logistic) * (2.0 + pre_gate * (1.0 - 2.0 * logistic))
        scale_one = back_grad * slope_one
        scale_two = back_grad * pre_up * slope_two
        one_ref[:, columns] = scale_one
        two_ref[:, columns] = scale_two
        along_gate = jnp.dot(v_rows[...], gate_t, preferred_element_type=F32)
        along_up = jnp.dot(v_rows[...], up_t, preferred_element_type=F32)
        ag_ref[:, columns] = along_gate
        au_ref[:, columns] = along_up
        out_gate[:, columns] = (scale_one * along_up + scale_two * along_gate).astype(BF16)
        out_up[:, columns] = (scale_one * along_gate).astype(BF16)
        return carry

    lax.fori_loop(0, 3, tile, 0)
    results_out(out_gate, out_up, gate_w, up_w, x_rows, swap, (out_a, out_b, out_c))


def first_expert(blocks, gate_w, up_w, down_w):
    message = jax.ShapeDtypeStruct((128, SUB, 256), BF16)
    hidden = jax.ShapeDtypeStruct((384, 768), F32)
    results = pl.pallas_call(
        first_expert_kernel,
        out_shape=[message] * 3 + [hidden] * 4,
        in_specs=[VM] * 3 + [ANY] * 3,
        out_specs=[VM] * 7,
        scratch_shapes=[pltpu.VMEM((4096, 768), BF16)] * 2
        + [pltpu.VMEM((768, 4096), BF16)]
        + [pltpu.VMEM((384, 4096), BF16)] * 3
        + [pltpu.VMEM((384, 768), BF16)] * 2
        + [pltpu.SemaphoreType.DMA((3,))],
        name="first_expert",
        compiler_params=pltpu.CompilerParams(vmem_limit_bytes=62 << 20),
    )(*blocks, gate_w, up_w, down_w)
    return results[:3], results[3:]


def first_scalars(total, entries):
    square = total[0:1, 0:1] / entries
    cross = total[1:2, 0:1] / entries
    image = total[2:3, 0:1] / entries
    norm_square = square + EPSILON
    norm = jnp.sqrt(norm_square)
    alpha = cross / norm_square
    variance = (image - 2.0 * alpha * cross + alpha * alpha * square) / norm_square
    beta = jnp.sqrt(jnp.maximum(variance, 0.0) + EPSILON)
    return {"norm": norm, "alpha": alpha, "beta": beta, "square": square}


def second_expert_kernel(
    entries, in_a, in_b, in_c, total, one_ref, two_ref, ag_ref, au_ref, gate_h, up_h, out_a, out_b, out_c,
    gate_w, up_w, v_rows, out_gate, out_up, sems,
):
    copies = [
        pltpu.make_async_copy(src, dst, sems.at[i])
        for i, (src, dst) in enumerate(((gate_h, gate_w), (up_h, up_w)))
    ]
    for copy in copies:
        copy.start()
    swap = swap_matrix()
    for r, source in enumerate((in_a, in_b, in_c)):
        unpack(source, 0, swap, v_rows, r * 128)
    scalars = first_scalars(total[...], entries)
    scale = 1.0 / (scalars["norm"] * scalars["beta"])
    shift = scalars["alpha"] * scale
    for copy in copies:
        copy.wait()

    def tile(index, carry):
        columns = pl.ds(pl.multiple_of(index * 256, 256), 256)
        along_gate = jnp.dot(v_rows[...], gate_w[:, columns], preferred_element_type=F32)
        along_up = jnp.dot(v_rows[...], up_w[:, columns], preferred_element_type=F32)
        along_gate = along_gate * scale - ag_ref[:, columns] * shift
        along_up = along_up * scale - au_ref[:, columns] * shift
        scale_one = one_ref[:, columns]
        out_gate[:, columns] = (scale_one * along_up + two_ref[:, columns] * along_gate).astype(BF16)
        out_up[:, columns] = (scale_one * along_gate).astype(BF16)
        return carry

    lax.fori_loop(0, 3, tile, 0)
    results_out(out_gate, out_up, gate_w, up_w, v_rows, swap, (out_a, out_b, out_c))


def second_expert(entries, blocks, total, hidden, gate_w, up_w):
    message = jax.ShapeDtypeStruct((128, SUB, 256), BF16)
    return pl.pallas_call(
        functools.partial(second_expert_kernel, entries),
        out_shape=[message] * 3,
        in_specs=[VM] * 8 + [ANY] * 2,
        out_specs=[VM] * 3,
        scratch_shapes=[pltpu.VMEM((4096, 768), BF16)] * 2
        + [pltpu.VMEM((384, 4096), BF16)]
        + [pltpu.VMEM((384, 768), BF16)] * 2
        + [pltpu.SemaphoreType.DMA((2,))],
        name="second_expert",
        compiler_params=pltpu.CompilerParams(vmem_limit_bytes=56 << 20),
    )(*blocks, total, *hidden, gate_w, up_w)


CONTRACT_FIRST = (((0,), (0,)), ((), ()))


def gather_image(blocks, pick_ref, swap, rows, image):
    for r in range(3):
        unpack(blocks[r], 0, swap, rows, r * 128)
    picks = jnp.concatenate([pick_ref[r] for r in range(3)], axis=0)
    for part in range(8):
        columns = slice(part * 512, (part + 1) * 512)
        image[:, columns] = lax.dot_general(picks, rows[:, columns], CONTRACT_FIRST, preferred_element_type=F32)


def as_tile(values):
    row = lax.broadcasted_iota(jnp.int32, (8, 128), 0)
    tile = jnp.zeros((8, 128), F32)
    for index, value in enumerate(values):
        tile = jnp.where(row == index, value, tile)
    return tile


def whole_sum(array):
    return jnp.sum(jnp.sum(array, axis=0, keepdims=True), axis=1, keepdims=True)


def turn_kernel(in_a, in_b, in_c, pick_ref, start, image, out_a, out_b, out_c, part_ref, rows):
    swap = swap_matrix()
    gather_image((in_a, in_b, in_c), pick_ref, swap, rows, image)
    anchor = start[...].astype(F32)
    found = image[...]
    part_ref[...] = as_tile([whole_sum(anchor * anchor), whole_sum(anchor * found), whole_sum(found * found)])
    for part in range(4):
        columns = slice(part * 1024, (part + 1) * 1024)
        narrow = image[:, columns].astype(BF16)
        for r in range(3):
            picked = jnp.dot(pick_ref[r], narrow, preferred_element_type=F32)
            rows[r * 128 : (r + 1) * 128, columns] = picked.astype(BF16)
    for r, out in enumerate((out_a, out_b, out_c)):
        pack(rows, r * 128, swap, out, 0)


def turn(blocks, pick, start):
    message = jax.ShapeDtypeStruct((128, SUB, 256), BF16)
    results = pl.pallas_call(
        turn_kernel,
        out_shape=[jax.ShapeDtypeStruct(start.shape, F32)]
        + [message] * 3
        + [jax.ShapeDtypeStruct((8, 128), F32)],
        in_specs=[VM] * 5,
        out_specs=[VM] * 5,
        scratch_shapes=[pltpu.VMEM((384, 4096), BF16)],
        name="turn",
        compiler_params=pltpu.CompilerParams(vmem_limit_bytes=32 << 20),
    )(*blocks, pick, start)
    return results[0], results[1:4], results[4]


def finish_kernel(
    entries, in_a, in_b, in_c, pick_ref, start, first_image, total_ref, basis_ref, residual_ref, tri_ref,
    rows, image, tile_a, tile_b, tile_c, sum_send, sum_recv,
):
    place = here()
    reduction = Reduction(place, (tile_a, tile_b, tile_c), sum_send, sum_recv)
    peers = []
    for axes in REDUCE_GROUPS:
        peers += [moved(place, axes, step) for step in offsets(axes)[1:]]
    entry_barrier(peers)
    swap = swap_matrix()
    gather_image((in_a, in_b, in_c), pick_ref, swap, rows, image)
    scalars = first_scalars(total_ref[...], entries)
    norm, alpha, beta = scalars["norm"], scalars["alpha"], scalars["beta"]
    base = start[...].astype(F32) / norm
    basis = ((first_image[...] / norm - alpha * base) / beta).astype(BF16)
    basis_ref[...] = basis
    wide = basis.astype(F32)
    found = image[...]
    partial = as_tile(
        [
            whole_sum(wide * found),
            whole_sum(found * found),
            whole_sum(base * found),
            whole_sum(wide * wide),
            whole_sum(wide * base),
            whole_sum(base * base),
        ]
    )
    reduction.send(0, partial)
    reduction.send(1, reduction.receive(0))
    reduction.send(2, reduction.receive(1))
    total = reduction.receive(2) / entries
    alpha_one = total[0:1, 0:1]
    square = (
        total[1:2, 0:1]
        - 2.0 * alpha_one * total[0:1, 0:1]
        - 2.0 * beta * total[2:3, 0:1]
        + alpha_one * alpha_one * total[3:4, 0:1]
        + 2.0 * alpha_one * beta * total[4:5, 0:1]
        + beta * beta * total[5:6, 0:1]
    )
    beta_two = jnp.sqrt(jnp.maximum(square, 0.0) + EPSILON)
    residual_ref[...] = image[...] - alpha_one * basis_ref[...].astype(F32) - beta * (start[...].astype(F32) / norm)
    tri_ref[...] = as_tile([alpha, beta, alpha_one, beta_two])


def finish(entries, blocks, pick, start, first_image, total):
    return pl.pallas_call(
        functools.partial(finish_kernel, entries),
        out_shape=[
            jax.ShapeDtypeStruct(start.shape, BF16),
            jax.ShapeDtypeStruct(start.shape, F32),
            jax.ShapeDtypeStruct((8, 128), F32),
        ],
        in_specs=[VM] * 7,
        out_specs=[VM] * 3,
        scratch_shapes=[pltpu.VMEM((384, 4096), BF16), pltpu.VMEM(start.shape, F32)] + reduction_scratch(),
        name="finish",
        compiler_params=pltpu.CompilerParams(
            collective_id=5, has_side_effects=True, vmem_limit_bytes=32 << 20
        ),
    )(*blocks, pick, start, first_image, total)


def on_device(tokens, cotangent, start, gates, routes, w_gate, w_up, w_down):
    entries = float(128 * tokens.shape[0] * tokens.shape[1])
    gate_w, up_w, down_w = w_gate[0], w_up[0], w_down[0]
    outgoing = send_messages(routes, gates, tokens, cotangent, start)
    blocks, pick = outgoing[:3], outgoing[3]
    arrived = exchange(blocks, False, 0)
    answers, hidden = first_expert(arrived, gate_w, up_w, down_w)
    returned = exchange(answers, True, 1)
    image_zero, blocks, part = turn(returned, pick, start)
    arrived, total = exchange(blocks, False, 2, part)
    answers = second_expert(entries, arrived, total, hidden, gate_w, up_w)
    returned = exchange(answers, True, 3)
    basis, residual, tri = finish(entries, returned, pick, start, image_zero, total)
    return basis, residual, tri[:4, 0]


def solution(mesh):
    rows = P(("dp", "expert"), None)
    experts = P(("dp", "expert"), None, None)
    return jax.shard_map(
        on_device,
        mesh=mesh,
        in_specs=(rows,) * 5 + (experts,) * 3,
        out_specs=(rows, rows, P()),
        check_vma=False,
    )
```

time: 753 us -> 376 us (0.50)
  blocking collectives: 430 us -> 0 us
  Pallas kernels: 0 us -> 352 us
  waiting for transfers between devices: 120 us -> 0 us
  matrix products: 84.8 us -> 0 us
  local copies, waits for them, and re-layouts: 81.6 us -> 22.6 us
  starting transfers between devices: 18.1 us -> 0 us
  other arithmetic: 7.9 us -> 0 us
    pallas_call x0 -> x9, Pallas kernels: none -> 352 us  [the longest x4 230 us: exchange(): pl.pallas_call(functools.partial(exchange_kernel, back, summing), out_sha...]
    psum x4 -> x0, blocking collectives: 251 us -> none  [the longest x2 125 us: residual_sum(): return lax.psum(jnp.sum(vector * vector), ('dp', 'expert'))]
    all_to_all x3 -> x0, blocking collectives: 179 us -> none  [the longest x2 120 us: send_back(): lax.all_to_all(flatten_four(block), ('dp', 'expert'), split_axis=0, conca...]
    all_to_all x2 -> x0, waiting for transfers between devices: 120 us -> none  [the longest x1 85.4 us: send_inputs(): lax.all_to_all(flatten_four(block), ('dp', 'expert'), split_axis=0, conca...]
    dot_general x16 -> x0, matrix products: 84.8 us -> none  [the longest x2 32.6 us: hessian_product(): jnp.einsum('sf,df->sd', out_gate, gate_w, preferred_element_type=jnp.floa...]
    all_to_all x10 -> x0, local copies, waits for them, and re-layouts: 79.4 us -> none  [the longest x4 27.6 us: send_back(): lax.all_to_all(flatten_four(block), ('dp', 'expert'), split_axis=0, conca...]
    unnamed x32 -> x42, local copies, waits for them, and re-layouts: 1.97 us -> 22 us
    all_to_all x2 -> x0, starting transfers between devices: 18.1 us -> none  [the longest x1 12 us: send_rows(): lax.all_to_all(flatten_four(block), ('dp', 'expert'), split_axis=0, conca...]
  transfers between devices with their start and end apart: 2 -> 0, of which waited for: 2 -> 0; matrix products, arithmetic and copies ran while one was open for 2% -> 0% of each run, Pallas kernels for 0% -> 0%
where the time goes in v1:
time: 376 us
  Pallas kernels  352 us (94%)
  local copies, waits for them, and re-layouts  22.6 us (6%)
    pallas_call x4, Pallas kernels, exchange(): pl.pallas_call(functools.partial(exchange_kernel, back, summing), out_sha...  230 us
    pallas_call x1, Pallas kernels, first_expert(): pl.pallas_call(first_expert_kernel, out_shape=[message] * 3 + [hidden] *...  46.5 us
    pallas_call x1, Pallas kernels, second_expert(): pl.pallas_call(functools.partial(second_expert_kernel, entries), out_shap...  27.8 us
    unnamed x42, local copies, waits for them, and re-layouts  22 us
    pallas_call x1, Pallas kernels, finish(): pl.pallas_call(functools.partial(finish_kernel, entries), out_shape=[jax....  18.8 us
    pallas_call x1, Pallas kernels, send_messages(): pl.pallas_call(send_kernel, out_shape=[message] * 3 + [jax.ShapeDtypeStru...  18.1 us
    pallas_call x1, Pallas kernels, turn(): pl.pallas_call(turn_kernel, out_shape=[jax.ShapeDtypeStruct(start.shape,...  11 us

profile of v1, /device:TPU:1, one launch (start us, length us, event | category | flops | bytes accessed | tf_op | source)
XLA Modules:
  0.0 375.8 jit_solution(4855345593330769697)
XLA Ops:
  0.6 0.0 copy-start.4
  0.6 0.9 copy-done.4
  1.6 0.0 copy-start.14
  1.6 0.9 copy-done.14
  2.5 0.0 copy-start.15
  2.5 0.9 copy-done.15
  3.5 0.0 copy-start.18
  3.5 0.7 copy-done.18
  4.2 0.0 copy-start.19
  4.2 0.7 copy-done.19
  4.9 18.1 %send_messages.1 = (bf16[128,16,768]{2,1,0:T(8,128)(2,1)S(1)}, bf16[128,16,768]{2,1,0:T(8,128)(2,1)S(1)}, bf16[128,16,768]{2,1,0:T(8,128)(2,1)S(1)}, bf16[3,128,32]{2,1,0:T(8,128)(2,1)S(1)}) custom-call(s32[8,32]{1,0:T(8,128)S(1)} %bitcast.49, f32[8,32]{1,0:T(8,128)S(1)} %bitcast.50, bf16[32,4096]{1,0:T(8,128)(2,1)S(1)} %copy-done.14, ...), custom_call_target="tpu_custom_call" | custom-call | tf_op jit(solution)/shard_map/send_messages/pallas_call | solution.py:358
  23.0 0.0 copy-start.1
  23.0 1.7 copy-done.1
  24.7 0.0 copy-start.2
  24.7 1.7 copy-done.2
  26.4 0.0 copy-start.3
  26.4 1.7 copy-done.3
  28.0 111.4 %exchange_0.1 = (bf16[8,4,4,16,768]{4,3,2,1,0:T(8,128)(2,1)S(1)}, bf16[8,4,4,16,768]{4,3,2,1,0:T(8,128)(2,1)}, bf16[8,4,4,16,768]{4,3,2,1,0:T(8,128)(2,1)}) custom-call(bf16[4,4,8,16,768]{4,3,2,1,0:T(8,128)(2,1)} %bitcast.30, bf16[4,4,8,16,768]{4,3,2,1,0:T(8,128)(2,1)} %bitcast.31, bf16[4,4,8,16,768]{4,3,2,1,0:T(8,128)(2,1)} %bitcast.32), custom_call_target="tpu_custom_call" | custom-call | tf_op jit(solution)/shard_map/exchange_0/pallas_call | solution.py:272
  139.4 0.0 copy-start
  139.4 1.7 copy-done
  141.1 46.5 %first_expert.1 = (bf16[128,16,256]{2,1,0:T(8,128)(2,1)}, bf16[128,16,256]{2,1,0:T(8,128)(2,1)}, bf16[128,16,256]{2,1,0:T(8,128)(2,1)}, f32[384,768]{1,0:T(8,128...) custom-call(bf16[128,16,768]{2,1,0:T(8,128)(2,1)} %bitcast.29, bf16[128,16,768]{2,1,0:T(8,128)(2,1)} %bitcast.56, ...), custom_call_target="tpu_custom_call" | custom-call | tf_op jit(solution)/shard_map/first_expert/pallas_call | solution.py:434
  187.7 0.0 copy-start.5
  187.7 0.0 copy-start.9
  187.7 1.3 copy-done.9
  189.0 0.0 copy-start.10
  189.0 1.2 copy-done.10
  190.2 39.7 %exchange_1.1 = (bf16[4,4,8,16,256]{4,3,2,1,0:T(8,128)(2,1)S(1)}, bf16[4,4,8,16,256]{4,3,2,1,0:T(8,128)(2,1)S(1)}, bf16[4,4,8,16,256]{4,3,2,1,0:T(8,128)(2,1)S(1)}) custom-call(bf16[8,4,4,16,256]{4,3,2,1,0:T(8,128)(2,1)S(1)} %bitcast.36, bf16[8,4,4,16,256]{4,3,2,1,0:T(8,128)(2,1)S(1)} %bitcast.37, bf16[8,4,4,16,256]{4,3,2,1,0:T(8,128)(2,1)} %bitcast.58), custom_call_target="tpu_custom_call" | custom-call | tf_op jit(solution)/shard_map/exchange_1/pallas_call | solution.py:272
  229.9 0.0 copy-done.5
  229.9 11.0 %turn.1 = (f32[32,4096]{1,0:T(8,128)S(1)}, bf16[128,16,256]{2,1,0:T(8,128)(2,1)S(1)}, bf16[128,16,256]{2,1,0:T(8,128)(2,1)S(1)}, bf16[128,16,256]{2,1,0:T(8,128)(2,1)S(1)}, f32[8,128]{1,0:T(8,128)S(1)}) custom-call(bf16[128,16,256]{2,1,0:T(8,128)(2,1)S(1)} %bitcast.46, bf16[128,16,256]{2,1,0:T(8,128)(2,1)S(1)} %bitcast.47, ...), custom_call_target="tpu_custom_call" | custom-call | tf_op jit(solution)/shard_map/turn/pallas_call | solution.py:554
  241.0 0.0 copy-start.13
  241.0 1.0 copy-done.13
  242.0 40.2 %exchange_2.1 = (bf16[8,4,4,16,256]{4,3,2,1,0:T(8,128)(2,1)S(1)}, bf16[8,4,4,16,256]{4,3,2,1,0:T(8,128)(2,1)S(1)}, bf16[8,4,4,16,256]{4,3,2,1,0:T(8,128)(2,1)S(1)}, f32[8,128]{1,0:T(8,128)S(1)}) custom-call(bf16[4,4,8,16,256]{4,3,2,1,0:T(8,128)(2,1)S(1)} %bitcast.43, bf16[4,4,8,16,256]{4,3,2,1,0:T(8,128)(2,1)S(1)} %bitcast.44, ...), custom_call_target="tpu_custom_call" | custom-call | tf_op jit(solution)/shard_map/exchange_2/pallas_call | solution.py:272
  282.2 0.0 copy-start.6
  282.2 1.0 copy-done.6
  283.3 1.0 copy-done.7
  284.2 1.0 copy-done.8
  285.2 0.6 copy-done.16
  285.8 27.8 %second_expert.1 = (bf16[128,16,256]{2,1,0:T(8,128)(2,1)}, bf16[128,16,256]{2,1,0:T(8,128)(2,1)}, bf16[128,16,256]{2,1,0:T(8,128)(2,1)}) custom-call(bf16[128,16,256]{2,1,0:T(8,128)(2,1)} %bitcast.33, bf16[128,16,256]{2,1,0:T(8,128)(2,1)} %bitcast.34, bf16[128,16,256]{2,1,0:T(8,128)(2,1)} %bitcast.35, f32[8,128]{1,0:T(8,128)} %copy-done.16, ...), custom_call_target="tpu_custom_call" | custom-call | tf_op jit(solution)/shard_map/second_expert/pallas_call | solution.py:498
  313.6 0.0 copy-start.17
  313.6 0.0 copy-start.11
  313.6 1.2 copy-done.11
  314.8 1.2 copy-done.12
  316.1 38.8 %exchange_3.1 = (bf16[4,4,8,16,256]{4,3,2,1,0:T(8,128)(2,1)S(1)}, bf16[4,4,8,16,256]{4,3,2,1,0:T(8,128)(2,1)S(1)}, bf16[4,4,8,16,256]{4,3,2,1,0:T(8,128)(2,1)S(1)}) custom-call(bf16[8,4,4,16,256]{4,3,2,1,0:T(8,128)(2,1)S(1)} %bitcast.38, bf16[8,4,4,16,256]{4,3,2,1,0:T(8,128)(2,1)S(1)} %bitcast.39, bf16[8,4,4,16,256]{4,3,2,1,0:T(8,128)(2,1)} %bitcast.59), custom_call_target="tpu_custom_call" | custom-call | tf_op jit(solution)/shard_map/exchange_3/pallas_call | solution.py:272
  354.8 0.0 copy-done.17
  354.9 18.8 %finish.1 = (bf16[32,4096]{1,0:T(8,128)(2,1)S(1)}, f32[32,4096]{1,0:T(8,128)S(1)}, f32[8,128]{1,0:T(8,128)S(1)}) custom-call(bf16[128,16,256]{2,1,0:T(8,128)(2,1)S(1)} %bitcast.40, bf16[128,16,256]{2,1,0:T(8,128)(2,1)S(1)} %bitcast.41, bf16[128,16,256]{2,1,0:T(8,128)(2,1)S(1)} %bitcast.42, bf16[3,128,32]{2,1,0:T(8,128)(2,1)S(1)} %get-tuple-element.50.pick_ref, ...), custom_call_target="tpu_custom_call" | custom-call | tf_op jit(solution)/shard_map/finish/pallas_call | solution.py:616
  373.7 0.6 slice_reduce_fusion
  374.3 0.7 copy.13
  375.0 0.8 copy.14
  (4 shorter events, 0.0 us)
Async XLA Ops:
  0.6 1.0 copy-start.4
  1.6 0.9 copy-start.14
  2.5 0.9 copy-start.15
  3.5 0.7 copy-start.18
  4.2 0.7 copy-start.19
  23.0 1.7 copy-start.1
  24.7 1.7 copy-start.2
  26.4 1.7 copy-start.3
  139.4 1.7 copy-start
  187.7 42.2 %copy-start.5 = (bf16[32,4096]{1,0:T(8,128)(2,1)S(1)}, bf16[32,4096]{1,0:T(8,128)(2,1)}, u32[]{:S(2)}) copy-start(bf16[32,4096]{1,0:T(8,128)(2,1)} %start.5) | copy-start | bytes 786436
  187.7 1.3 copy-start.9
  189.0 1.2 copy-start.10
  241.0 1.0 copy-start.13
  282.2 1.0 copy-start.6
  283.3 1.0 copy-start.7
  284.2 1.0 copy-start.8
  285.2 0.6 copy-start.16
  313.6 41.3 %copy-start.17 = (f32[8,128]{1,0:T(8,128)S(1)}, f32[8,128]{1,0:T(8,128)}, u32[]{:S(2)}) copy-start(f32[8,128]{1,0:T(8,128)} %copy-done.16) | copy-start | bytes 12292
  313.6 1.2 copy-start.11
  314.8 1.2 copy-start.12

commit v2 on v1

--- a/solution.py
+++ b/solution.py
@@ -326,44 +326,195 @@
     return value["z"] * 32 + value["x"] * 8 + value["y"] * 2 + rem(position, 2)
 
 
-def send_kernel(routes, gates, tokens, cotangent, start, out_a, out_b, out_c, pick_ref, rows):
+def own_picks(table, pick_ref, early):
+    for r in range(3):
+        ids = expert_ids(ORDERS[r]).astype(F32)
+        named = jnp.zeros((128, 32), F32)
+        for k in range(8):
+            named = named + (table[k : k + 1, 0:32] == ids).astype(F32)
+        before = jnp.dot(named.astype(BF16), early, preferred_element_type=F32)
+        keep = (named > 0.5) & (before == float(r))
+        pick_ref[r] = keep.astype(F32).astype(BF16)
+
+
+def scatter_kernel(
+    tokens, cotangent, start, table_ref, out_a, out_b, out_c, pick_ref,
+    held, tables, first_a, first_b, first_c, second_a, second_b, second_c, rows,
+    row_send, row_recv, tab_send, tab_recv, send_two, recv_two, local_two, send_three, recv_three, local_three,
+):
+    sources, outs = (tokens, cotangent, start), (out_a, out_b, out_c)
+    first_hold, second_hold = (first_a, first_b, first_c), (second_a, second_b, second_c)
+    place = here()
+    plans = [groups_of(order, False) for order in ORDERS]
+    entry_barrier(peers_of(place))
+
+    def remote(src, dst, send_sem, recv_sem, target):
+        return pltpu.make_async_remote_copy(
+            src, dst, send_sem, recv_sem, device_id=device_of(target), device_id_type=MESH
+        )
+
+    for step in offsets(("z",))[1:]:
+        for u, (one, two, three) in enumerate(plans):
+            mine, target, slot = index_of(place, one), moved(place, one, step), slot_id(one, step)
+            remote(table_ref, tables.at[u, mine], tab_send.at[u], tab_recv.at[u, slot], target).start()
+            remote(sources[u], held.at[u, mine], row_send.at[u], row_recv.at[u, slot], target).start()
+
     swap = swap_matrix()
     early = lax.broadcasted_iota(jnp.int32, (32, 32), 0) < lax.broadcasted_iota(jnp.int32, (32, 32), 1)
     early = early.astype(F32).astype(BF16)
-    for r, out in enumerate((out_a, out_b, out_c)):
-        ids = expert_ids(ORDERS[r])
-        named = jnp.zeros((128, 32), F32)
-        weight = jnp.zeros((128, 32), F32)
+    position = lax.broadcasted_iota(jnp.int32, (32, 32), 0)
+
+    def origin_of(turn, u):
+        step = offsets(plans[u][0])[turn]
+        return step, moved(place, plans[u][0], step, -1)
+
+    def build(turn, u, between):
+        order = ORDERS[u]
+        step, origin = origin_of(turn, u)
+        source = place[order[0]] if turn == 0 else origin[order[0]]
+        if turn == 0:
+            table, block = table_ref, sources[u]
+        else:
+            table, block = tables.at[u, source], held.at[u, source]
+            remote(table, table, tab_send.at[u], tab_recv.at[u, step[0]], origin).wait_recv()
+            remote(block, block, row_send.at[u], row_recv.at[u, step[0]], origin).wait_recv()
+        value = {order[0]: place[order[0]], order[1]: position // 8, order[2]: rem(position // 2, 4)}
+        ids = (value["z"] * 32 + value["x"] * 8 + value["y"] * 2 + rem(position, 2)).astype(F32)
+        named = jnp.zeros((32, 32), F32)
+        weight = jnp.zeros((32, 32), F32)
         for k in range(8):
-            hit = routes[k : k + 1, :] == ids
+            hit = table[k : k + 1, 0:32] == ids
             named = named + hit.astype(F32)
-            weight = weight + jnp.where(hit, gates[k : k + 1, :], 0.0)
+            weight = weight + jnp.where(hit, table[8 + k : 9 + k, 0:32], 0.0)
         before = jnp.dot(named.astype(BF16), early, preferred_element_type=F32)
-        keep = (named > 0.5) & (before == float(r))
-        pick = keep.astype(F32).astype(BF16)
-        pick_ref[r] = pick
-        slot_gate = jnp.sum(jnp.where(keep, weight, 0.0), axis=1, keepdims=True)
-        for unit, source in enumerate((tokens, cotangent, start)):
-            for part in range(4):
-                columns = slice(part * 1024, (part + 1) * 1024)
-                picked = jnp.dot(pick, source[:, columns], preferred_element_type=F32)
-                if unit == 1:
-                    picked = picked * slot_gate
-                rows[:, columns] = picked.astype(BF16)
-            pack(rows, 0, swap, out, unit * 256)
-
-
-def send_messages(routes, gates, tokens, cotangent, start):
-    message = jax.ShapeDtypeStruct((128, SUB, 768), BF16)
-    return pl.pallas_call(
-        send_kernel,
-        out_shape=[message] * 3 + [jax.ShapeDtypeStruct((3, 128, 32), BF16)],
-        in_specs=[VM] * 5,
-        out_specs=[VM] * 4,
-        scratch_shapes=[pltpu.VMEM((128, 4096), BF16)],
-        name="send_messages",
-        compiler_params=pltpu.CompilerParams(vmem_limit_bytes=32 << 20),
-    )(routes.T, gates.T, tokens, cotangent, start)
+        keeps = [((named > 0.5) & (before == float(r))).astype(F32) for r in range(3)]
+        pick = jnp.concatenate(keeps, axis=0)
+        slot_gate = jnp.sum(pick * jnp.concatenate([weight] * 3, axis=0), axis=1, keepdims=True)
+        pick = pick.astype(BF16)
+        for part in range(4):
+            columns = slice(part * 1024, (part + 1) * 1024)
+            picked = jnp.dot(pick, block[:, columns], preferred_element_type=F32)
+            if u == 1:
+                picked = picked * slot_gate
+            rows[:, columns] = picked.astype(BF16)
+        between()
+
+        def turned(r, carry):
+            lanes = pl.ds(pl.multiple_of(r * 256, 256), 256)
+            for half in range(2):
+                begin = pl.multiple_of(r * 32 + half * 16, 16)
+                stacked = jnp.concatenate(
+                    [rows[pl.ds(begin, 16), j * 256 : (j + 1) * 256] for j in range(SUB)], axis=0
+                )
+                tile = jnp.dot(swap, stacked, preferred_element_type=F32).astype(BF16)
+                first_hold[u][source, half * 2 : half * 2 + 2, :, :, lanes] = tile.reshape(2, 8, SUB, 256)
+            return carry
+
+        lax.fori_loop(0, 3, turned, 0)
+
+    def send(turn, u):
+        one, two, three = plans[u]
+        source = index_of(origin_of(turn, u)[1], one) if turn else index_of(place, one)
+        mine_two = index_of(place, two)
+        for hop in offsets(two)[1:]:
+            target = moved(place, two, hop)
+            remote(
+                first_hold[u].at[source, index_of(target, two)],
+                second_hold[u].at[mine_two, source],
+                send_two.at[u],
+                recv_two.at[u, slot_id(two, hop)],
+                target,
+            ).start()
+        pltpu.make_async_copy(
+            first_hold[u].at[source, mine_two], second_hold[u].at[mine_two, source], local_two.at[u]
+        ).start()
+
+    chunks = [(turn, u) for turn in range(4) for u in range(3)]
+    for index, chunk in enumerate(chunks):
+        build(*chunk, (lambda: None) if index == 0 else functools.partial(send, *chunks[index - 1]))
+    own_picks(table_ref, pick_ref, early)
+    send(*chunks[-1])
+    for turn in range(4):
+        for u, (one, two, three) in enumerate(plans):
+            step = offsets(two)[turn]
+            mine_two, mine_three = index_of(place, two), index_of(place, three)
+            if turn == 0:
+                source = mine_two
+                block = second_hold[u].at[source]
+                pltpu.make_async_copy(block, block, local_two.at[u]).wait()
+            else:
+                origin = moved(place, two, step, -1)
+                source = index_of(origin, two)
+                block = second_hold[u].at[source]
+                remote(block, block, send_two.at[u], recv_two.at[u, slot_id(two, step)], origin).wait_recv()
+            for hop in offsets(three)[1:]:
+                target = moved(place, three, hop)
+                remote(
+                    second_hold[u].at[source, :, index_of(target, three)],
+                    outs[u].at[mine_three, source],
+                    send_three.at[u],
+                    recv_three.at[u],
+                    target,
+                ).start()
+            pltpu.make_async_copy(
+                second_hold[u].at[source, :, mine_three], outs[u].at[mine_three, source], local_three.at[u]
+            ).start()
+    near = moved(place, ("c",), (1,))
+    for u, (one, two, three) in enumerate(plans):
+        rest = tables.at[u, pl.ds(0, 3)]
+        remote(rest, rest, tab_send.at[u], recv_three.at[u], near).wait_send()
+        rest = held.at[u, pl.ds(0, 3)]
+        remote(rest, rest, row_send.at[u], recv_three.at[u], near).wait_send()
+        rest = second_hold[u].at[pl.ds(0, 3)]
+        remote(rest, rest, send_two.at[u], recv_three.at[u], near).wait_send()
+        rest = outs[u].at[pl.ds(0, 7)]
+        bulk = remote(rest, rest, send_three.at[u], recv_three.at[u], near)
+        bulk.wait_send()
+        bulk.wait_recv()
+        mine = outs[u].at[index_of(place, three)]
+        pltpu.make_async_copy(mine, mine, local_three.at[u]).wait()
+
+
+def scatter(routes, gates, tokens, cotangent, start):
+    table = jnp.concatenate([routes.T.astype(F32), gates.T], axis=0)
+    table = jnp.pad(table, ((0, 0), (0, 96)))
+    results = pl.pallas_call(
+        scatter_kernel,
+        out_shape=[jax.ShapeDtypeStruct((8, 4, 4, SUB, 768), BF16)] * 3
+        + [jax.ShapeDtypeStruct((3, 128, 32), BF16)],
+        in_specs=[VM] * 4,
+        out_specs=[ANY] * 3 + [VM],
+        scratch_shapes=[pltpu.VMEM((3, 4, 32, 4096), BF16), pltpu.VMEM((3, 4, 16, 128), F32)]
+        + [pltpu.VMEM((4, 4, 8, SUB, 768), BF16)] * 6
+        + [pltpu.VMEM((96, 4096), BF16)]
+        + [pltpu.SemaphoreType.DMA((3,)), pltpu.SemaphoreType.DMA((3, 4))] * 2
+        + [pltpu.SemaphoreType.DMA((3,)), pltpu.SemaphoreType.DMA((3, 8))]
+        + [pltpu.SemaphoreType.DMA((3,))] * 4,
+        name="scatter",
+        compiler_params=pltpu.CompilerParams(
+            collective_id=0, has_side_effects=True, vmem_limit_bytes=48 << 20
+        ),
+    )(tokens, cotangent, start, table)
+    return [result.reshape(128, SUB, 768) for result in results[:3]], results[3]
+
+
+def unpack_unit(in_ref, u, r, swap, rows_ref):
+    order, home = ORDERS[r], ORDERS[u]
+
+    def block(index, carry):
+        pieces = []
+        for spot in range(16):
+            value = {order[2]: index // 2, order[1]: spot // 4, order[0]: spot % 4}
+            third = value[home[2]] * 2 + rem(index, 2)
+            pieces.append(in_ref[third * 16 + value[home[1]] * 4 + value[home[0]], :, r * 256 : (r + 1) * 256])
+        stacked = jnp.concatenate(pieces, axis=0)
+        turned = jnp.dot(swap, stacked, preferred_element_type=F32).astype(BF16)
+        start = pl.multiple_of(r * 128 + index * 16, 16)
+        for j in range(SUB):
+            rows_ref[pl.ds(start, 16), j * 256 : (j + 1) * 256] = turned[j * 16 : (j + 1) * 16, :]
+        return carry
+
+    lax.fori_loop(0, 8, block, 0)
 
 
 CONTRACT_LAST = (((1,), (1,)), ((), ()))
@@ -397,9 +548,9 @@
     for copy in copies:
         copy.start()
     swap = swap_matrix()
-    for r, source in enumerate((in_a, in_b, in_c)):
-        for unit, rows in enumerate((x_rows, c_rows, v_rows)):
-            unpack(source, unit * 256, swap, rows, r * 128)
+    for u, (source, rows) in enumerate(((in_a, x_rows), (in_b, c_rows), (in_c, v_rows))):
+        for r in range(3):
+            unpack_unit(source, u, r, swap, rows)
     for copy in copies:
         copy.wait()
 
@@ -633,9 +784,7 @@
 def on_device(tokens, cotangent, start, gates, routes, w_gate, w_up, w_down):
     entries = float(128 * tokens.shape[0] * tokens.shape[1])
     gate_w, up_w, down_w = w_gate[0], w_up[0], w_down[0]
-    outgoing = send_messages(routes, gates, tokens, cotangent, start)
-    blocks, pick = outgoing[:3], outgoing[3]
-    arrived = exchange(blocks, False, 0)
+    arrived, pick = scatter(routes, gates, tokens, cotangent, start)
     answers, hidden = first_expert(arrived, gate_w, up_w, down_w)
     returned = exchange(answers, True, 1)
     image_zero, blocks, part = turn(returned, pick, start)

time: 376 us -> 331 us (0.88)
  Pallas kernels: 352 us -> 312 us
  local copies, waits for them, and re-layouts: 22.6 us -> 16.2 us
    pallas_call x4 -> x3, Pallas kernels: 230 us -> 119 us  [exchange(): pl.pallas_call(functools.partial(exchange_kernel, back, summing), out_sha...]
    pallas_call x1, Pallas kernels: 18.1 us -> 89.1 us  [scatter(): pl.pallas_call(scatter_kernel, out_shape=[jax.ShapeDtypeStruct((8, 4, 4,...]
    unnamed x42 -> x32, local copies, waits for them, and re-layouts: 22 us -> 15.5 us
where the time goes in v2:
time: 331 us; the launch traced here: 330 us
  Pallas kernels  312 us (94%)
  local copies, waits for them, and re-layouts  16.2 us (5%)
    pallas_call x3, Pallas kernels, exchange(): pl.pallas_call(functools.partial(exchange_kernel, back, summing), out_sha...  119 us
    pallas_call x1, Pallas kernels, scatter(): pl.pallas_call(scatter_kernel, out_shape=[jax.ShapeDtypeStruct((8, 4, 4,...  89.1 us
    pallas_call x1, Pallas kernels, first_expert(): pl.pallas_call(first_expert_kernel, out_shape=[message] * 3 + [hidden] *...  46.6 us
    pallas_call x1, Pallas kernels, second_expert(): pl.pallas_call(functools.partial(second_expert_kernel, entries), out_shap...  27.8 us
    pallas_call x1, Pallas kernels, finish(): pl.pallas_call(functools.partial(finish_kernel, entries), out_shape=[jax....  18.5 us
    unnamed x32, local copies, waits for them, and re-layouts  15.5 us
    pallas_call x1, Pallas kernels, turn(): pl.pallas_call(turn_kernel, out_shape=[jax.ShapeDtypeStruct(start.shape,...  10.9 us

profile of v2, /device:TPU:1, one launch (start us, length us, event | category | flops | bytes accessed | tf_op | source)
XLA Modules:
  0.0 330.3 jit_solution(17532711107895326717)
XLA Ops:
  0.6 0.7 convert_bitcast_fusion
  1.3 0.7 select_maximum_fusion.table_ref
  2.0 0.0 copy-start.1
  2.0 0.9 copy-done.1
  3.0 0.0 copy-start.11
  3.0 0.9 copy-done.11
  3.9 0.0 copy-start.12
  3.9 0.9 copy-done.12
  4.9 89.1 %scatter.1 = (bf16[8,4,4,16,768]{4,3,2,1,0:T(8,128)(2,1)S(1)}, bf16[8,4,4,16,768]{4,3,2,1,0:T(8,128)(2,1)}, bf16[8,4,4,16,768]{4,3,2,1,0:T(8,128)(2,1)}, bf16[3,128,32]{2,1,0:T(8,128)(2,1)S(1)}) custom-call(bf16[32,4096]{1,0:T(8,128)(2,1)S(1)} %copy-done.11, bf16[32,4096]{1,0:T(8,128)(2,1)S(1)} %copy-done.12, bf16[32,4096]{1,0:T(8,128)(2,1)S(1)} %copy-done.1, ...), custom_call_target="tpu_custom_call" | custom-call | tf_op jit(solution)/shard_map/scatter/pallas_call | solution.py:481
  93.9 0.0 copy-start
  93.9 1.7 copy-done
  95.7 46.6 %first_expert.1 = (bf16[128,16,256]{2,1,0:T(8,128)(2,1)}, bf16[128,16,256]{2,1,0:T(8,128)(2,1)}, bf16[128,16,256]{2,1,0:T(8,128)(2,1)}, f32[384,768]{1,0:T(8,128...) custom-call(bf16[128,16,768]{2,1,0:T(8,128)(2,1)} %bitcast.27, bf16[128,16,768]{2,1,0:T(8,128)(2,1)} %bitcast.49, ...), custom_call_target="tpu_custom_call" | custom-call | tf_op jit(solution)/shard_map/first_expert/pallas_call | solution.py:585
  142.3 0.0 copy-start.2
  142.3 0.0 copy-start.6
  142.3 1.3 copy-done.6
  143.6 0.0 copy-start.7
  143.6 1.2 copy-done.7
  144.8 39.7 %exchange_1.1 = (bf16[4,4,8,16,256]{4,3,2,1,0:T(8,128)(2,1)S(1)}, bf16[4,4,8,16,256]{4,3,2,1,0:T(8,128)(2,1)S(1)}, bf16[4,4,8,16,256]{4,3,2,1,0:T(8,128)(2,1)S(1)}) custom-call(bf16[8,4,4,16,256]{4,3,2,1,0:T(8,128)(2,1)S(1)} %bitcast.31, bf16[8,4,4,16,256]{4,3,2,1,0:T(8,128)(2,1)S(1)} %bitcast.32, bf16[8,4,4,16,256]{4,3,2,1,0:T(8,128)(2,1)} %bitcast.51), custom_call_target="tpu_custom_call" | custom-call | tf_op jit(solution)/shard_map/exchange_1/pallas_call | solution.py:272
  184.5 0.0 copy-done.2
  184.5 10.9 %turn.1 = (f32[32,4096]{1,0:T(8,128)S(1)}, bf16[128,16,256]{2,1,0:T(8,128)(2,1)S(1)}, bf16[128,16,256]{2,1,0:T(8,128)(2,1)S(1)}, bf16[128,16,256]{2,1,0:T(8,128)(2,1)S(1)}, f32[8,128]{1,0:T(8,128)S(1)}) custom-call(bf16[128,16,256]{2,1,0:T(8,128)(2,1)S(1)} %bitcast.41, bf16[128,16,256]{2,1,0:T(8,128)(2,1)S(1)} %bitcast.42, ...), custom_call_target="tpu_custom_call" | custom-call | tf_op jit(solution)/shard_map/turn/pallas_call | solution.py:705
  195.3 0.0 copy-start.10
  195.4 1.0 copy-done.10
  196.3 40.2 %exchange_2.1 = (bf16[8,4,4,16,256]{4,3,2,1,0:T(8,128)(2,1)S(1)}, bf16[8,4,4,16,256]{4,3,2,1,0:T(8,128)(2,1)S(1)}, bf16[8,4,4,16,256]{4,3,2,1,0:T(8,128)(2,1)S(1)}, f32[8,128]{1,0:T(8,128)S(1)}) custom-call(bf16[4,4,8,16,256]{4,3,2,1,0:T(8,128)(2,1)S(1)} %bitcast.38, bf16[4,4,8,16,256]{4,3,2,1,0:T(8,128)(2,1)S(1)} %bitcast.39, ...), custom_call_target="tpu_custom_call" | custom-call | tf_op jit(solution)/shard_map/exchange_2/pallas_call | solution.py:272
  236.6 0.0 copy-start.3
  236.6 1.0 copy-done.3
  237.6 0.0 copy-start.4
  237.6 1.0 copy-done.4
  238.6 0.0 copy-start.5
  238.6 1.0 copy-done.5
  239.5 0.0 copy-start.13
  239.5 0.6 copy-done.13
  240.1 27.8 %second_expert.1 = (bf16[128,16,256]{2,1,0:T(8,128)(2,1)}, bf16[128,16,256]{2,1,0:T(8,128)(2,1)}, bf16[128,16,256]{2,1,0:T(8,128)(2,1)}) custom-call(bf16[128,16,256]{2,1,0:T(8,128)(2,1)} %bitcast.28, bf16[128,16,256]{2,1,0:T(8,128)(2,1)} %bitcast.29, bf16[128,16,256]{2,1,0:T(8,128)(2,1)} %bitcast.30, f32[8,128]{1,0:T(8,128)} %copy-done.13, ...), custom_call_target="tpu_custom_call" | custom-call | tf_op jit(solution)/shard_map/second_expert/pallas_call | solution.py:649
  268.0 0.0 copy-start.14
  268.0 0.0 copy-start.8
  268.0 1.2 copy-done.8
  269.2 0.0 copy-start.9
  269.2 1.2 copy-done.9
  270.4 39.2 %exchange_3.1 = (bf16[4,4,8,16,256]{4,3,2,1,0:T(8,128)(2,1)S(1)}, bf16[4,4,8,16,256]{4,3,2,1,0:T(8,128)(2,1)S(1)}, bf16[4,4,8,16,256]{4,3,2,1,0:T(8,128)(2,1)S(1)}) custom-call(bf16[8,4,4,16,256]{4,3,2,1,0:T(8,128)(2,1)S(1)} %bitcast.33, bf16[8,4,4,16,256]{4,3,2,1,0:T(8,128)(2,1)S(1)} %bitcast.34, bf16[8,4,4,16,256]{4,3,2,1,0:T(8,128)(2,1)} %bitcast.52), custom_call_target="tpu_custom_call" | custom-call | tf_op jit(solution)/shard_map/exchange_3/pallas_call | solution.py:272
  309.7 0.0 copy-done.14
  309.7 18.5 %finish.1 = (bf16[32,4096]{1,0:T(8,128)(2,1)S(1)}, f32[32,4096]{1,0:T(8,128)S(1)}, f32[8,128]{1,0:T(8,128)S(1)}) custom-call(bf16[128,16,256]{2,1,0:T(8,128)(2,1)S(1)} %bitcast.35, bf16[128,16,256]{2,1,0:T(8,128)(2,1)S(1)} %bitcast.36, bf16[128,16,256]{2,1,0:T(8,128)(2,1)S(1)} %bitcast.37, bf16[3,128,32]{2,1,0:T(8,128)(2,1)S(1)} %get-tuple-element.44.pick_ref, ...), custom_call_target="tpu_custom_call" | custom-call | tf_op jit(solution)/shard_map/finish/pallas_call | solution.py:767
  328.2 0.6 slice_reduce_fusion
  328.8 0.7 copy.13
  329.5 0.8 copy.14
Async XLA Ops:
  2.0 0.9 copy-start.1
  3.0 0.9 copy-start.11
  3.9 0.9 copy-start.12
  93.9 1.7 copy-start
  142.3 42.2 %copy-start.2 = (bf16[32,4096]{1,0:T(8,128)(2,1)S(1)}, bf16[32,4096]{1,0:T(8,128)(2,1)}, u32[]{:S(2)}) copy-start(bf16[32,4096]{1,0:T(8,128)(2,1)} %start.5) | copy-start | bytes 786436
  142.3 1.3 copy-start.6
  143.6 1.2 copy-start.7
  195.3 1.0 copy-start.10
  236.6 1.0 copy-start.3
  237.6 1.0 copy-start.4
  238.6 1.0 copy-start.5
  239.5 0.6 copy-start.13
  268.0 41.7 %copy-start.14 = (f32[8,128]{1,0:T(8,128)S(1)}, f32[8,128]{1,0:T(8,128)}, u32[]{:S(2)}) copy-start(f32[8,128]{1,0:T(8,128)} %copy-done.13) | copy-start | bytes 12292
  268.0 1.2 copy-start.8
  269.2 1.2 copy-start.9

commit v3 on v2

--- a/solution.py
+++ b/solution.py
@@ -77,11 +77,19 @@
     return found
 
 
-def entry_barrier(places):
+def greet(places):
     barrier = pltpu.get_barrier_semaphore()
     for place in places:
         pl.semaphore_signal(barrier, inc=1, device_id=device_of(place), device_id_type=MESH)
-    pl.semaphore_wait(barrier, len(places))
+
+
+def await_greetings(places):
+    pl.semaphore_wait(pltpu.get_barrier_semaphore(), len(places))
+
+
+def entry_barrier(places):
+    greet(places)
+    await_greetings(places)
 
 
 REDUCE_GROUPS = (("z",), ("x",), ("y", "c"))
@@ -138,47 +146,45 @@
     ]
 
 
-def exchange_kernel(back, summing, *refs):
-    blocks = refs[:3]
-    refs = refs[3:]
-    if summing:
-        part, refs = refs[0], refs[1:]
-    outs, refs = refs[:3], refs[3:]
-    if summing:
-        total, refs = refs[0], refs[1:]
-    first_hold, second_hold, refs = refs[:3], refs[3:6], refs[6:]
-    (send_one, send_two, send_three, recv_one, recv_two, recv_three, local_one, local_two, local_three) = refs[:9]
-    place = here()
+def exchange_steps(place, back, make, outs, net, reduction=None, part=None):
+    blocks, first_hold, second_hold = net[:3], net[3:6], net[6:9]
+    (send_one, send_two, send_three, recv_one, recv_two, recv_three, local_one, local_two, local_three) = net[9:18]
     plans = [groups_of(order, back) for order in ORDERS]
-    if summing:
-        tiles, (sum_send, sum_recv) = refs[9:12], refs[12:14]
-        reduction = Reduction(place, tiles, sum_send, sum_recv)
-    entry_barrier(peers_of(place))
+    summing = reduction is not None
 
     def remote(src, dst, send_sem, recv_sem, target):
         return pltpu.make_async_remote_copy(
             src, dst, send_sem, recv_sem, device_id=device_of(target), device_id_type=MESH
         )
 
+    def launch(turn, r):
+        one = plans[r][0]
+        step = offsets(one)[turn]
+        mine = index_of(place, one)
+        if turn == 0:
+            pltpu.make_async_copy(blocks[r].at[mine], first_hold[r].at[mine], local_one.at[r]).start()
+            return
+        target = moved(place, one, step)
+        remote(
+            blocks[r].at[index_of(target, one)],
+            first_hold[r].at[mine],
+            send_one.at[r],
+            recv_one.at[r, slot_id(one, step)],
+            target,
+        ).start()
+
     if summing:
-        reduction.send(0, part[...])
-    for turn in range(8):
-        for r, (one, two, three) in enumerate(plans):
-            if turn >= size_of(one):
-                continue
-            step = offsets(one)[turn]
-            mine = index_of(place, one)
-            if turn == 0:
-                pltpu.make_async_copy(blocks[r].at[mine], first_hold[r].at[mine], local_one.at[r]).start()
-                continue
-            target = moved(place, one, step)
-            remote(
-                blocks[r].at[index_of(target, one)],
-                first_hold[r].at[mine],
-                send_one.at[r],
-                recv_one.at[r, slot_id(one, step)],
-                target,
-            ).start()
+        reduction.send(0, part)
+    chunks = [
+        (turn, r) for turn in (1, 2, 3, 4, 5, 6, 7, 0) for r in range(3) if turn < size_of(plans[r][0])
+    ]
+    for number, (turn, r) in enumerate(chunks):
+        one = plans[r][0]
+        target = moved(place, one, offsets(one)[turn])
+        make(r, index_of(target, one), blocks[r])
+        if number:
+            launch(*chunks[number - 1])
+    launch(*chunks[-1])
     for turn in range(8):
         for r, (one, two, three) in enumerate(plans):
             if turn >= size_of(one):
@@ -234,7 +240,7 @@
             ).start()
     if summing:
         reduction.send(2, reduction.receive(1))
-        total[...] = reduction.receive(2)
+        total = reduction.receive(2)
     near = moved(place, ("c",), (1,))
     for r, (one, two, three) in enumerate(plans):
         rest = blocks[r].at[pl.ds(0, size_of(one) - 1)]
@@ -247,41 +253,25 @@
         bulk.wait_recv()
         mine = outs[r].at[index_of(place, three)]
         pltpu.make_async_copy(mine, mine, local_three.at[r]).wait()
-
-
-def exchange(blocks, back, number, part=None):
-    sub, lanes = blocks[0].shape[1:]
-    dims_in = (8, 4, 4) if back else (4, 4, 8)
-    dims_out = dims_in[::-1]
-    one, two, three = dims_in
-    summing = part is not None
-    scratch = [pltpu.VMEM((one, two, three, sub, lanes), BF16)] * 3
-    scratch += [pltpu.VMEM((two, one, three, sub, lanes), BF16)] * 3
+    return total if summing else None
+
+
+def net_scratch(back):
+    dims = (8, 4, 4) if back else (4, 4, 8)
+    held = (dims[1], dims[0], dims[2])
+    scratch = [pltpu.VMEM(dims + (SUB, 256), BF16)] * 6 + [pltpu.VMEM(held + (SUB, 256), BF16)] * 3
     scratch += [pltpu.SemaphoreType.DMA((3,))] * 3
     scratch += [pltpu.SemaphoreType.DMA((3, 8))] * 2
-    scratch += [pltpu.SemaphoreType.DMA((3,))] * 4
-    out_shape = [jax.ShapeDtypeStruct(dims_out + (sub, lanes), BF16)] * 3
-    operands = [block.reshape(dims_in + (sub, lanes)) for block in blocks]
-    in_specs, out_specs = [ANY] * 3, [ANY] * 3
-    if summing:
-        operands.append(part)
-        in_specs.append(VM)
-        out_specs.append(VM)
-        out_shape.append(jax.ShapeDtypeStruct((8, 128), F32))
-        scratch += reduction_scratch()
-    results = pl.pallas_call(
-        functools.partial(exchange_kernel, back, summing),
-        out_shape=out_shape,
-        in_specs=in_specs,
-        out_specs=out_specs,
-        scratch_shapes=scratch,
-        name="exchange_%d" % number,
-        compiler_params=pltpu.CompilerParams(
-            collective_id=number, has_side_effects=True, vmem_limit_bytes=48 << 20
-        ),
-    )(*operands)
-    moved_blocks = [result.reshape(128, sub, lanes) for result in results[:3]]
-    return (moved_blocks, results[3]) if summing else moved_blocks
+    return scratch + [pltpu.SemaphoreType.DMA((3,))] * 4
+
+
+def arriving(back):
+    dims = (4, 4, 8) if back else (8, 4, 4)
+    return [jax.ShapeDtypeStruct(dims + (SUB, 256), BF16)] * 3
+
+
+def as_messages(blocks):
+    return [block.reshape(128, SUB, 256) for block in blocks]
 
 
 def swap_matrix():
@@ -291,17 +281,24 @@
     return hit.astype(F32).astype(BF16)
 
 
-def pack(rows_ref, row_start, swap, out_ref, lane):
-    def block(index, carry):
-        start = pl.multiple_of(row_start + index * 16, 16)
-        stacked = jnp.concatenate(
-            [rows_ref[pl.ds(start, 16), j * 256 : (j + 1) * 256] for j in range(SUB)], axis=0
-        )
-        turned = jnp.dot(swap, stacked, preferred_element_type=F32).astype(BF16)
-        out_ref[pl.ds(pl.multiple_of(index * 16, 16), 16), :, lane : lane + 256] = turned.reshape(16, 16, 256)
-        return carry
-
-    lax.fori_loop(0, 8, block, 0)
+def turned_rows(rows_ref, start, swap):
+    start = pl.multiple_of(start, 16)
+    stacked = jnp.concatenate(
+        [rows_ref[pl.ds(start, 16), j * 256 : (j + 1) * 256] for j in range(SUB)], axis=0
+    )
+    return jnp.dot(swap, stacked, preferred_element_type=F32).astype(BF16)
+
+
+def maker(back, rows_ref, swap):
+    def make(r, index, block):
+        if back:
+            block[index] = turned_rows(rows_ref, r * 128 + index * 16, swap).reshape(4, 4, SUB, 256)
+            return
+        for half in range(2):
+            turned = turned_rows(rows_ref, r * 128 + index * 32 + half * 16, swap)
+            block[index, half * 2 : half * 2 + 2] = turned.reshape(2, 8, SUB, 256)
+
+    return make
 
 
 def unpack(in_ref, lane, swap, rows_ref, row_start):
@@ -524,7 +521,7 @@
     return lax.dot_general(left, right, CONTRACT_LAST, preferred_element_type=F32)
 
 
-def results_out(out_gate, out_up, gate_w, up_w, rows, swap, outs):
+def results_out(out_gate, out_up, gate_w, up_w, rows):
     def tile(index, carry):
         start = pl.multiple_of(index * 256, 256)
         summed = last_dot(out_gate[...], gate_w[pl.ds(start, 256), :])
@@ -533,14 +530,14 @@
         return carry
 
     lax.fori_loop(0, 16, tile, 0)
-    for r in range(3):
-        pack(rows, r * 128, swap, outs[r], 0)
 
 
 def first_expert_kernel(
     in_a, in_b, in_c, gate_h, up_h, down_h, out_a, out_b, out_c, one_ref, two_ref, ag_ref, au_ref,
-    gate_w, up_w, down_w, x_rows, c_rows, v_rows, out_gate, out_up, sems,
+    gate_w, up_w, down_w, x_rows, c_rows, v_rows, out_gate, out_up, sems, *net,
 ):
+    place = here()
+    greet(peers_of(place))
     copies = [
         pltpu.make_async_copy(src, dst, sems.at[i])
         for i, (src, dst) in enumerate(((gate_h, gate_w), (up_h, up_w), (down_h, down_w)))
@@ -576,26 +573,30 @@
         return carry
 
     lax.fori_loop(0, 3, tile, 0)
-    results_out(out_gate, out_up, gate_w, up_w, x_rows, swap, (out_a, out_b, out_c))
+    results_out(out_gate, out_up, gate_w, up_w, x_rows)
+    await_greetings(peers_of(place))
+    exchange_steps(place, True, maker(True, x_rows, swap), (out_a, out_b, out_c), net)
 
 
 def first_expert(blocks, gate_w, up_w, down_w):
-    message = jax.ShapeDtypeStruct((128, SUB, 256), BF16)
     hidden = jax.ShapeDtypeStruct((384, 768), F32)
     results = pl.pallas_call(
         first_expert_kernel,
-        out_shape=[message] * 3 + [hidden] * 4,
+        out_shape=arriving(True) + [hidden] * 4,
         in_specs=[VM] * 3 + [ANY] * 3,
-        out_specs=[VM] * 7,
+        out_specs=[ANY] * 3 + [VM] * 4,
         scratch_shapes=[pltpu.VMEM((4096, 768), BF16)] * 2
         + [pltpu.VMEM((768, 4096), BF16)]
         + [pltpu.VMEM((384, 4096), BF16)] * 3
         + [pltpu.VMEM((384, 768), BF16)] * 2
-        + [pltpu.SemaphoreType.DMA((3,))],
+        + [pltpu.SemaphoreType.DMA((3,))]
+        + net_scratch(True),
         name="first_expert",
-        compiler_params=pltpu.CompilerParams(vmem_limit_bytes=62 << 20),
+        compiler_params=pltpu.CompilerParams(
+            collective_id=1, has_side_effects=True, vmem_limit_bytes=62 << 20
+        ),
     )(*blocks, gate_w, up_w, down_w)
-    return results[:3], results[3:]
+    return as_messages(results[:3]), results[3:]
 
 
 def first_scalars(total, entries):
@@ -612,8 +613,10 @@
 
 def second_expert_kernel(
     entries, in_a, in_b, in_c, total, one_ref, two_ref, ag_ref, au_ref, gate_h, up_h, out_a, out_b, out_c,
-    gate_w, up_w, v_rows, out_gate, out_up, sems,
+    gate_w, up_w, v_rows, out_gate, out_up, sems, *net,
 ):
+    place = here()
+    greet(peers_of(place))
     copies = [
         pltpu.make_async_copy(src, dst, sems.at[i])
         for i, (src, dst) in enumerate(((gate_h, gate_w), (up_h, up_w)))
@@ -641,23 +644,28 @@
         return carry
 
     lax.fori_loop(0, 3, tile, 0)
-    results_out(out_gate, out_up, gate_w, up_w, v_rows, swap, (out_a, out_b, out_c))
+    results_out(out_gate, out_up, gate_w, up_w, v_rows)
+    await_greetings(peers_of(place))
+    exchange_steps(place, True, maker(True, v_rows, swap), (out_a, out_b, out_c), net)
 
 
 def second_expert(entries, blocks, total, hidden, gate_w, up_w):
-    message = jax.ShapeDtypeStruct((128, SUB, 256), BF16)
-    return pl.pallas_call(
+    results = pl.pallas_call(
         functools.partial(second_expert_kernel, entries),
-        out_shape=[message] * 3,
+        out_shape=arriving(True),
         in_specs=[VM] * 8 + [ANY] * 2,
-        out_specs=[VM] * 3,
+        out_specs=[ANY] * 3,
         scratch_shapes=[pltpu.VMEM((4096, 768), BF16)] * 2
         + [pltpu.VMEM((384, 4096), BF16)]
         + [pltpu.VMEM((384, 768), BF16)] * 2
-        + [pltpu.SemaphoreType.DMA((2,))],
+        + [pltpu.SemaphoreType.DMA((2,))]
+        + net_scratch(True),
         name="second_expert",
-        compiler_params=pltpu.CompilerParams(vmem_limit_bytes=56 << 20),
+        compiler_params=pltpu.CompilerParams(
+            collective_id=3, has_side_effects=True, vmem_limit_bytes=56 << 20
+        ),
     )(*blocks, total, *hidden, gate_w, up_w)
+    return as_messages(results)
 
 
 CONTRACT_FIRST = (((0,), (0,)), ((), ()))
@@ -684,36 +692,45 @@
     return jnp.sum(jnp.sum(array, axis=0, keepdims=True), axis=1, keepdims=True)
 
 
-def turn_kernel(in_a, in_b, in_c, pick_ref, start, image, out_a, out_b, out_c, part_ref, rows):
+def turn_kernel(
+    in_a, in_b, in_c, pick_ref, start, image, out_a, out_b, out_c, total_ref, rows, tile_a, tile_b, tile_c,
+    sum_send, sum_recv, *net,
+):
+    place = here()
+    greet(peers_of(place))
     swap = swap_matrix()
     gather_image((in_a, in_b, in_c), pick_ref, swap, rows, image)
     anchor = start[...].astype(F32)
     found = image[...]
-    part_ref[...] = as_tile([whole_sum(anchor * anchor), whole_sum(anchor * found), whole_sum(found * found)])
-    for part in range(4):
-        columns = slice(part * 1024, (part + 1) * 1024)
+    part = as_tile([whole_sum(anchor * anchor), whole_sum(anchor * found), whole_sum(found * found)])
+    for quarter in range(4):
+        columns = slice(quarter * 1024, (quarter + 1) * 1024)
         narrow = image[:, columns].astype(BF16)
         for r in range(3):
             picked = jnp.dot(pick_ref[r], narrow, preferred_element_type=F32)
             rows[r * 128 : (r + 1) * 128, columns] = picked.astype(BF16)
-    for r, out in enumerate((out_a, out_b, out_c)):
-        pack(rows, r * 128, swap, out, 0)
+    await_greetings(peers_of(place))
+    reduction = Reduction(place, (tile_a, tile_b, tile_c), sum_send, sum_recv)
+    total_ref[...] = exchange_steps(
+        place, False, maker(False, rows, swap), (out_a, out_b, out_c), net, reduction, part
+    )
 
 
 def turn(blocks, pick, start):
-    message = jax.ShapeDtypeStruct((128, SUB, 256), BF16)
     results = pl.pallas_call(
         turn_kernel,
         out_shape=[jax.ShapeDtypeStruct(start.shape, F32)]
-        + [message] * 3
+        + arriving(False)
         + [jax.ShapeDtypeStruct((8, 128), F32)],
         in_specs=[VM] * 5,
-        out_specs=[VM] * 5,
-        scratch_shapes=[pltpu.VMEM((384, 4096), BF16)],
+        out_specs=[VM] + [ANY] * 3 + [VM],
+        scratch_shapes=[pltpu.VMEM((384, 4096), BF16)] + reduction_scratch() + net_scratch(False),
         name="turn",
-        compiler_params=pltpu.CompilerParams(vmem_limit_bytes=32 << 20),
+        compiler_params=pltpu.CompilerParams(
+            collective_id=2, has_side_effects=True, vmem_limit_bytes=40 << 20
+        ),
     )(*blocks, pick, start)
-    return results[0], results[1:4], results[4]
+    return results[0], as_messages(results[1:4]), results[4]
 
 
 def finish_kernel(
@@ -785,12 +802,9 @@
     entries = float(128 * tokens.shape[0] * tokens.shape[1])
     gate_w, up_w, down_w = w_gate[0], w_up[0], w_down[0]
     arrived, pick = scatter(routes, gates, tokens, cotangent, start)
-    answers, hidden = first_expert(arrived, gate_w, up_w, down_w)
-    returned = exchange(answers, True, 1)
-    image_zero, blocks, part = turn(returned, pick, start)
-    arrived, total = exchange(blocks, False, 2, part)
-    answers = second_expert(entries, arrived, total, hidden, gate_w, up_w)
-    returned = exchange(answers, True, 3)
+    returned, hidden = first_expert(arrived, gate_w, up_w, down_w)
+    image_zero, arrived, total = turn(returned, pick, start)
+    returned = second_expert(entries, arrived, total, hidden, gate_w, up_w)
     basis, residual, tri = finish(entries, returned, pick, start, image_zero, total)
     return basis, residual, tri[:4, 0]
 

time: 331 us -> 315 us (0.952)
  Pallas kernels: 312 us -> 294 us
    pallas_call x4 -> x1, Pallas kernels: 166 us -> 80.8 us  [first_expert(): pl.pallas_call(first_expert_kernel, out_shape=arriving(True) + [hidden] *...]
    pallas_call x1, Pallas kernels: 10.9 us -> 44.3 us  [turn(): pl.pallas_call(turn_kernel, out_shape=[jax.ShapeDtypeStruct(start.shape,...]
    pallas_call x1, Pallas kernels: 27.8 us -> 60.4 us  [second_expert(): pl.pallas_call(functools.partial(second_expert_kernel, entries), out_shap...]
    unnamed x32 -> x34, local copies, waits for them, and re-layouts: 15.5 us -> 16.9 us
where the time goes in v3:
time: 315 us; the launch traced here: 314 us
  Pallas kernels  294 us (93%)
  local copies, waits for them, and re-layouts  17.5 us (6%)
    pallas_call x1, Pallas kernels, scatter(): pl.pallas_call(scatter_kernel, out_shape=[jax.ShapeDtypeStruct((8, 4, 4,...  89.1 us
    pallas_call x1, Pallas kernels, first_expert(): pl.pallas_call(first_expert_kernel, out_shape=arriving(True) + [hidden] *...  80.8 us
    pallas_call x1, Pallas kernels, second_expert(): pl.pallas_call(functools.partial(second_expert_kernel, entries), out_shap...  60.4 us
    pallas_call x1, Pallas kernels, turn(): pl.pallas_call(turn_kernel, out_shape=[jax.ShapeDtypeStruct(start.shape,...  44.3 us
    pallas_call x1, Pallas kernels, finish(): pl.pallas_call(functools.partial(finish_kernel, entries), out_shape=[jax....  19.7 us
    unnamed x34, local copies, waits for them, and re-layouts  16.9 us

profile of v3, /device:TPU:1, one launch (start us, length us, event | category | flops | bytes accessed | tf_op | source)
XLA Modules:
  0.0 314.0 jit_solution(4930340998158091012)
XLA Ops:
  0.6 0.7 convert_bitcast_fusion
  1.3 0.7 select_maximum_fusion.table_ref
  2.0 0.0 copy-start.1
  2.0 0.9 copy-done.1
  3.0 0.0 copy-start.12
  3.0 0.9 copy-done.12
  3.9 0.0 copy-start.13
  3.9 0.9 copy-done.13
  4.9 89.1 %scatter.1 = (bf16[8,4,4,16,768]{4,3,2,1,0:T(8,128)(2,1)S(1)}, bf16[8,4,4,16,768]{4,3,2,1,0:T(8,128)(2,1)}, bf16[8,4,4,16,768]{4,3,2,1,0:T(8,128)(2,1)}, bf16[3,128,32]{2,1,0:T(8,128)(2,1)S(1)}) custom-call(bf16[32,4096]{1,0:T(8,128)(2,1)S(1)} %copy-done.12, bf16[32,4096]{1,0:T(8,128)(2,1)S(1)} %copy-done.13, bf16[32,4096]{1,0:T(8,128)(2,1)S(1)} %copy-done.1, ...), custom_call_target="tpu_custom_call" | custom-call | tf_op jit(solution)/shard_map/scatter/pallas_call | solution.py:478
  93.9 0.0 copy-start
  93.9 1.7 copy-done
  95.6 0.0 copy-start.2
  95.6 80.8 %first_expert.1 = (bf16[4,4,8,16,256]{4,3,2,1,0:T(8,128)(2,1)}, bf16[4,4,8,16,256]{4,3,2,1,0:T(8,128)(2,1)}, bf16[4,4,8,16,256]{4,3,2,1,0:T(8,128)(2,1)}, f32[38...) custom-call(bf16[128,16,768]{2,1,0:T(8,128)(2,1)} %bitcast.18, ...), custom_call_target="tpu_custom_call" | custom-call | tf_op jit(solution)/shard_map/first_expert/pallas_call | solution.py:583
  176.5 0.0 copy-done.2
  176.5 0.0 copy-start.9
  176.5 1.2 copy-done.9
  177.7 0.0 copy-start.10
  177.7 1.2 copy-done.10
  178.9 0.0 copy-start.11
  178.9 1.2 copy-done.11
  180.2 44.3 %turn.1 = (f32[32,4096]{1,0:T(8,128)S(1)}, bf16[8,4,4,16,256]{4,3,2,1,0:T(8,128)(2,1)S(1)}, bf16[8,4,4,16,256]{4,3,2,1,0:T(8,128)(2,1)S(1)}, bf16[8,4,4,16,256]{4,3,2,1,0:T(8,128)(2,1)S(1)}, f32[8,128]{1,0:T(8,128)S(1)}) custom-call(bf16[128,16,256]{2,1,0:T(8,128)(2,1)S(1)} %bitcast.25, bf16[128,16,256]{2,1,0:T(8,128)(2,1)S(1)} %bitcast.26, ...), custom_call_target="tpu_custom_call" | custom-call | tf_op jit(solution)/shard_map/turn/pallas_call | solution.py:720
  224.5 0.0 copy-start.6
  224.5 1.0 copy-done.6
  225.5 0.0 copy-start.7
  225.5 1.0 copy-done.7
  226.5 0.0 copy-start.8
  226.5 1.0 copy-done.8
  227.5 0.0 copy-start.14
  227.5 0.6 copy-done.14
  228.1 0.0 copy-start.15
  228.1 60.4 %second_expert.1 = (bf16[4,4,8,16,256]{4,3,2,1,0:T(8,128)(2,1)}, bf16[4,4,8,16,256]{4,3,2,1,0:T(8,128)(2,1)}, bf16[4,4,8,16,256]{4,3,2,1,0:T(8,128)(2,1)}) custom-call(bf16[128,16,256]{2,1,0:T(8,128)(2,1)} %bitcast.22, bf16[128,16,256]{2,1,0:T(8,128)(2,1)} %bitcast.23, bf16[128,16,256]{2,1,0:T(8,128)(2,1)} %bitcast.24, f32[8,128]{1,0:T(8,128)} %copy-done.14, ...), custom_call_target="tpu_custom_call" | custom-call | tf_op jit(solution)/shard_map/second_expert/pallas_call | solution.py:653
  288.5 0.0 copy-done.15
  288.5 0.0 copy-start.3
  288.5 1.2 copy-done.3
  289.7 0.0 copy-start.4
  289.7 1.2 copy-done.4
  290.9 0.0 copy-start.5
  290.9 1.2 copy-done.5
  292.1 19.7 %finish.1 = (bf16[32,4096]{1,0:T(8,128)(2,1)S(1)}, f32[32,4096]{1,0:T(8,128)S(1)}, f32[8,128]{1,0:T(8,128)S(1)}) custom-call(bf16[128,16,256]{2,1,0:T(8,128)(2,1)S(1)} %bitcast.19, bf16[128,16,256]{2,1,0:T(8,128)(2,1)S(1)} %bitcast.20, bf16[128,16,256]{2,1,0:T(8,128)(2,1)S(1)} %bitcast.21, bf16[3,128,32]{2,1,0:T(8,128)(2,1)S(1)} %get-tuple-element.31.pick_ref, ...), custom_call_target="tpu_custom_call" | custom-call | tf_op jit(solution)/shard_map/finish/pallas_call | solution.py:784
  311.9 0.6 slice_reduce_fusion
  312.5 0.7 copy.13
  313.2 0.8 copy.14
Async XLA Ops:
  2.0 0.9 copy-start.1
  3.0 0.9 copy-start.12
  3.9 0.9 copy-start.13
  93.9 1.7 copy-start
  95.6 80.9 %copy-start.2 = (bf16[32,4096]{1,0:T(8,128)(2,1)S(1)}, bf16[32,4096]{1,0:T(8,128)(2,1)}, u32[]{:S(2)}) copy-start(bf16[32,4096]{1,0:T(8,128)(2,1)} %start.5) | copy-start | bytes 786436
  176.5 1.2 copy-start.9
  177.7 1.2 copy-start.10
  178.9 1.2 copy-start.11
  224.5 1.0 copy-start.6
  225.5 1.0 copy-start.7
  226.5 1.0 copy-start.8
  227.5 0.6 copy-start.14
  228.1 60.4 %copy-start.15 = (f32[8,128]{1,0:T(8,128)S(1)}, f32[8,128]{1,0:T(8,128)}, u32[]{:S(2)}) copy-start(f32[8,128]{1,0:T(8,128)} %copy-done.14) | copy-start | bytes 12292
  288.5 1.2 copy-start.3
  289.7 1.2 copy-start.4
  290.9 1.2 copy-start.5
